TPU v7x, 256 devices: a whole 4x4x8 slice. The times are simulated.
256 devices in a mesh: gx: 8 (over z), gy: 4 (over x), gz: 8 (over y, core).
Axes of the slice: x: 4, y: 4, z: 8, core: 2. Of those that a mesh axis runs over, the one named last changes fastest.
Arguments:
- electric: float32 [3, 64, 64, 1024], P(None, 'gx', 'gy', 'gz'), may hold values from -6 to 6
- permittivity_class: int32 [64, 64, 1024], P('gx', 'gy', 'gz'), may hold values from 0 to 3
- cell_index: int32 [8, 1024, 128], P('gx', ('gy', 'gz')), may hold values from 0 to 16384, as said below
- polarization: float32 [2, 3, 8, 1024, 128], P(None, None, 'gx', ('gy', 'gz')), may hold values from -3 to 3
- populations: float32 [2, 8, 1024, 128], P(None, 'gx', ('gy', 'gz')), may hold values from 0.05 to 0.45
- resonance: float32 [8, 1024, 128], P('gx', ('gy', 'gz')), may hold values from 0.5 to 1.5
- dephasing: float32 [8, 1024, 128], P('gx', ('gy', 'gz')), may hold values from 0.05 to 0.8
- coupling: float32 [8, 1024, 128], P('gx', ('gy', 'gz')), may hold values from 0.1 to 1
- pump_rate: float32 [8, 1024, 128], P('gx', ('gy', 'gz')), may hold values from 0.02 to 0.4
Outputs:
- electric_out: float32 [3, 64, 64, 1024], P(None, 'gx', 'gy', 'gz')
- magnetic_out: float32 [3, 64, 64, 1024], P(None, 'gx', 'gy', 'gz')
- polarization_out: float32 [2, 3, 8, 1024, 128], P(None, None, 'gx', ('gy', 'gz'))
- populations_out: float32 [2, 8, 1024, 128], P(None, 'gx', ('gy', 'gz'))
Inputs may be any that keep to these rules, and one draw needn't show every extreme that they name: `cell_index`: A value below 16384 names the local cell (x 16 + y) * 128 + z of the target block; 16384 marks an empty slot. Every owner's buckets toward the devices of one index of gy, drawn from the seed, are full; each other bucket has an empty last slot.
All inputs are finite; a program needn't handle non-finite values.
Results may differ from a plain program's by a relative error of at most 0.0001.
Values sent between devices are 32-bit elements; how exact they have to be, the bound alone decides.
A program may use at most 64 MiB of HBM per device.

v0:
```python
import jax
import jax.numpy as jnp
from jax import lax
from jax.sharding import PartitionSpec as P

STEPS = 4


time_step = 0.5
pump_decay = 0.2
upper_decay = 0.02
work_share = 0.05
class_permittivity = (1.0, 2.1, 6.0, 12.25)


def extended_2(block, sides, width):
    for axis, dim in sides:
        count = lax.axis_size(axis)
        forward = [(i, i + 1) for i in range(count - 1)]
        backward = [(target, source) for source, target in forward]
        low = lax.ppermute(
            lax.slice_in_dim(block, block.shape[dim] - width, None, axis=dim), axis, forward
        )
        high = lax.ppermute(lax.slice_in_dim(block, 0, width, axis=dim), axis, backward)
        block = jnp.concatenate([low, block, high], axis=dim)
    return block


def inverse_permittivity(classes):
    inverse = jnp.zeros(classes.shape, jnp.float32)
    for number, epsilon in enumerate(class_permittivity):
        inverse = inverse + jnp.where(classes == number, 1.0 / epsilon, 0.0)
    return inverse


def combine_curl(along_x, along_y, along_z):
    return jnp.stack([along_y[2] - along_z[1], along_z[0] - along_x[2], along_x[1] - along_y[0]])


def bloch_update(
    sample, current, previous, upper, pumped, resonance, dephasing, coupling, pump_rate
):
    lower = 1.0 - upper - pumped
    damping = 0.5 * time_step * dephasing
    stiffness = resonance * time_step * (resonance * time_step)
    advanced = (
        (2.0 - stiffness) * current
        - (1.0 - damping) * previous
        + coupling * (time_step * time_step) * (lower - upper) * sample
    ) / (1.0 + damping)
    work = jnp.sum(sample * (advanced - previous), axis=0) / (2.0 * time_step)
    pumped_next = pumped + time_step * (pump_rate * lower - pump_decay * pumped)
    upper_next = upper + time_step * (
        pump_decay * pumped - upper_decay * upper + work_share * work / resonance
    )
    return (advanced, current, upper_next, pumped_next)


def shards(
    electric,
    permittivity_class,
    cell_index,
    polarization,
    populations,
    resonance,
    dephasing,
    coupling,
    pump_rate,
):
    width_x, width_y, width_z = (electric.shape[1], electric.shape[2], electric.shape[3])
    cell_count = width_x * width_y * width_z
    bucket_count = cell_index.shape[1]
    slot_count = cell_index.shape[2]
    inverse = inverse_permittivity(permittivity_class)
    received = lax.all_to_all(cell_index, ("gy", "gz"), split_axis=1, concat_axis=1, tiled=True)
    safe_index = jnp.minimum(received, cell_count - 1).reshape(-1)
    weight = (received < cell_count).reshape(-1).astype(jnp.float32)
    dropped = received.reshape(-1)
    pos_x = lax.broadcasted_iota(jnp.int32, (1, width_x + 1, 1, 1), 1)
    pos_y = lax.broadcasted_iota(jnp.int32, (1, 1, width_y + 1, 1), 2)
    pos_z = lax.broadcasted_iota(jnp.int32, (1, 1, 1, width_z + 1), 3)
    keep_x = jnp.where((pos_x == 0) & (lax.axis_index("gx") == 0), 0.0, 1.0)
    keep_y = jnp.where((pos_y == 0) & (lax.axis_index("gy") == 0), 0.0, 1.0)
    keep_z = jnp.where((pos_z == 0) & (lax.axis_index("gz") == 0), 0.0, 1.0)
    boundary = keep_x * keep_y * keep_z
    extended = jnp.zeros((3, width_x + 1, width_y + 1, width_z + 1), jnp.float32)
    current = polarization[0]
    previous = polarization[1]
    upper = populations[0]
    pumped = populations[1]
    for repeat in range(STEPS):
        padded = extended_2(electric, (("gx", 1), ("gy", 2), ("gz", 3)), 1)
        base = padded[:, :-1, :-1, :-1]
        advance_curl = combine_curl(
            padded[:, 1:, :-1, :-1] - base,
            padded[:, :-1, 1:, :-1] - base,
            padded[:, :-1, :-1, 1:] - base,
        )
        extended = (extended - time_step * advance_curl) * boundary
        sample = lax.all_to_all(
            (electric.reshape(3, -1)[:, safe_index] * weight).reshape(
                3, 1, bucket_count, slot_count
            ),
            ("gy", "gz"),
            split_axis=2,
            concat_axis=2,
            tiled=True,
        )
        advanced, previous, upper, pumped = bloch_update(
            sample, current, previous, upper, pumped, resonance, dephasing, coupling, pump_rate
        )
        change = advanced - previous
        current = advanced
        returned = lax.all_to_all(change, ("gy", "gz"), split_axis=2, concat_axis=2, tiled=True)
        flat_change = returned.reshape(3, -1)
        summed = (
            jnp.zeros((3, cell_count), jnp.float32).at[:, dropped].add(flat_change, mode="drop")
        )
        inner = extended[:, 1:, 1:, 1:]
        curl = combine_curl(
            inner - extended[:, :-1, 1:, 1:],
            inner - extended[:, 1:, :-1, 1:],
            inner - extended[:, 1:, 1:, :-1],
        )
        electric = electric + inverse * (
            time_step * curl - summed.reshape(3, width_x, width_y, width_z)
        )
    polar_out = jnp.stack([current, previous])
    popul_out = jnp.stack([upper, pumped])
    return (electric, extended[:, 1:, 1:, 1:], polar_out, popul_out)


def solution(mesh):
    return jax.shard_map(
        shards,
        mesh=mesh,
        in_specs=(
            P(None, "gx", "gy", "gz"),
            P("gx", "gy", "gz"),
            P("gx", ("gy", "gz"), None),
            P(None, None, "gx", ("gy", "gz"), None),
            P(None, "gx", ("gy", "gz"), None),
            P("gx", ("gy", "gz"), None),
            P("gx", ("gy", "gz"), None),
            P("gx", ("gy", "gz"), None),
            P("gx", ("gy", "gz"), None),
        ),
        out_specs=(
            P(None, "gx", "gy", "gz"),
            P(None, "gx", "gy", "gz"),
            P(None, None, "gx", ("gy", "gz"), None),
            P(None, "gx", ("gy", "gz"), None),
        ),
        check_vma=False,
    )
```

profile of v0, /device:TPU:1, one launch (start us, length us, event | category | flops | bytes accessed | tf_op | source)
XLA Modules:
  0.0 427.6 jit_solution(9170665439001395123)
XLA Ops:
  0.6 8.7 %all-to-all-start = ((s32[1,32,128]{2,0,1:T(1,128)}), s32[1,32,128]{2,0,1:T(1,128)S(1)}, u32[]{:S(2)}, u32[]{:S(2)}) async-start(s32[1,32,128]{2,0,1:T(1,128)} %bitcast.220), calls=%async_computation | async-start | bytes 32768 | tf_op jit(solution)/shard_map/all_to_all | solution.py:75
  10.1 3.5 collective-permute-start
  13.7 1.3 collective-permute-start.1
  17.6 5.6 %copy.158 = f32[3,8,16,128]{0,3,2,1:T(8,128)} copy(f32[3,8,16,128]{3,2,1,0:T(8,128)} %param.9) | data formatting | bytes 393216 | tf_op args[0]
  24.0 1.3 collective-permute-start.3
  25.3 4.0 collective-permute-start.2
  29.3 14.2 %gather_fusion = f32[4096,3]{1,0:T(8,128)S(1)} fusion(f32[3,16384]{0,1:T(8,128)} %bitcast.190, s32[4096]{0:T(1024)S(1)} %broadcast_clamp_fusion), kind=kCustom, calls=%fused_computation | custom fusion | bytes 114688 | tf_op jit(solution)/shard_map/gather | solution.py:101
  44.3 4.4 %collective-permute-start.4 = (f32[3,10,18,1]{3,2,1,0:T(8,128)S(1)}, f32[3,10,18,1]{3,2,1,0:T(8,128)S(1)}, u32[]{:S(2)}, u32[]{:S(2)}) collective-permute-start(f32[3,10,18,1]{3,2,1,0:T(8,128)S(1)} %get-tuple-element.81), channel_id=1, source_target_pairs={{0,1},{1,2},{2,3},{3,4},{4,5},{5,6},{6,7},{8,9},{9,10},{10,11},{11... | collective-permute-start | bytes 6488 | tf_op jit(solution)/shard_map/ppermute | solution.py:21
  49.4 6.7 %all-to-all-start.1 = ((f32[3,1,32,128]{3,1,0,2:T(1,128)}), f32[3,1,32,128]{3,1,0,2:T(1,128)S(1)}, u32[]{:S(2)}, u32[]{:S(2)}) async-start(f32[3,1,32,128]{3,1,0,2:T(1,128)} %broadcast_multiply_fusion.4), calls=%async_computation.1 | async-start | bytes 98304 | tf_op jit(solution)/shard_map/all_to_all | solution.py:100
  56.0 2.1 collective-permute-start.5
  58.6 6.4 %collective-permute-done.5 = f32[3,10,18,1]{3,2,1,0:T(8,128)S(1)} collective-permute-done((f32[3,10,18,1]{3,2,1,0:T(8,128)S(1)}, f32[3,10,18,1]{3,2,1,0:T(8,128)S(1)}, u32[]{:S(2)}, u32[]{:S(2)}) %collective-permute-start.5) | collective-permute-done | bytes 2192 | tf_op jit(solution)/shard_map/ppermute | solution.py:24
  67.0 6.9 %all-to-all-start.2 = ((f32[3,1,32,128]{3,1,0,2:T(1,128)}), f32[3,1,32,128]{3,1,0,2:T(1,128)S(1)}, u32[]{:S(2)}, u32[]{:S(2)}) async-start(f32[3,1,32,128]{3,1,0,2:T(1,128)} %copy.161), calls=%async_computation.2 | async-start | bytes 98304 | tf_op jit(solution)/shard_map/all_to_all | solution.py:114
  74.7 6.6 %all-to-all-done.2 = f32[3,1,32,128]{3,1,0,2:T(1,128)S(1)} async-done(((f32[3,1,32,128]{3,1,0,2:T(1,128)}), f32[3,1,32,128]{3,1,0,2:T(1,128)S(1)}, u32[]{:S(2)}, u32[]{:S(2)}) %all-to-all-start.2) | async-done | bytes 49184 | tf_op jit(solution)/shard_map/all_to_all | solution.py:114
  82.0 26.3 %scatter_custom_fusion = f32[3,16384]{0,1:T(8,128)} fusion(s32[4096]{0:T(1024)} %bitcast.216, f32[4096,3]{1,0:T(8,128)S(1)} %copy.163, f32[]{:T(128)} %constant.22.clone.1), kind=kCustom, calls=%fused_computation.14 | custom fusion | flops 12288 | bytes 197120 | tf_op jit(solution)/shard_map/scatter-add | solution.py:117
  108.4 5.3 %copy.164 = f32[3,8,16,128]{3,2,1,0:T(8,128)S(1)} copy(f32[3,8,16,128]{0,3,2,1:T(8,128)} %bitcast.187) | data formatting | bytes 393216 | tf_op jit(solution)/shard_map/reshape | solution.py:126
  113.8 1.3 collective-permute-start.7
  115.1 4.9 %collective-permute-start.6 = (f32[3,1,16,128]{3,2,1,0:T(8,128)S(1)}, f32[3,1,16,128]{3,2,1,0:T(8,128)S(1)}, u32[]{:S(2)}, u32[]{:S(2)}) collective-permute-start(f32[3,1,16,128]{3,2,1,0:T(8,128)S(1)} %get-tuple-element.103), channel_id=1, source_target_pairs={{0,32},{32,64},{64,96},{96,128},{128,160},{160,192},{192,224},{1,3... | collective-permute-start | bytes 73736 | tf_op jit(solution)/shard_map/ppermute | solution.py:21
  121.0 1.3 collective-permute-start.9
  122.3 4.0 collective-permute-start.8
  126.9 4.7 %copy.166 = f32[3,8,16,128]{0,3,2,1:T(8,128)} copy(f32[3,8,16,128]{3,2,1,0:T(8,128)S(1)} %fusion.22) | data formatting | bytes 393216 | tf_op jit(solution)/shard_map/add | solution.py:125
  131.6 14.2 %gather_fusion.1 = f32[4096,3]{1,0:T(8,128)S(1)} fusion(f32[3,16384]{0,1:T(8,128)} %bitcast.192, s32[4096]{0:T(1024)S(1)} %broadcast_clamp_fusion), kind=kCustom, calls=%fused_computation.1 | custom fusion | bytes 114688 | tf_op jit(solution)/shard_map/gather | solution.py:101
  146.6 3.9 collective-permute-start.10
  150.5 1.4 broadcast_multiply_fusion.3
  151.9 4.3 %all-to-all-start.3 = ((f32[3,1,32,128]{3,1,0,2:T(1,128)}), f32[3,1,32,128]{3,1,0,2:T(1,128)S(1)}, u32[]{:S(2)}, u32[]{:S(2)}) async-start(f32[3,1,32,128]{3,1,0,2:T(1,128)} %broadcast_multiply_fusion.3), calls=%async_computation.3 | async-start | bytes 98304 | tf_op jit(solution)/shard_map/all_to_all | solution.py:100
  156.2 2.1 collective-permute-start.11
  158.8 6.4 %collective-permute-done.11 = f32[3,10,18,1]{3,2,1,0:T(8,128)S(1)} collective-permute-done((f32[3,10,18,1]{3,2,1,0:T(8,128)S(1)}, f32[3,10,18,1]{3,2,1,0:T(8,128)S(1)}, u32[]{:S(2)}, u32[]{:S(2)}) %collective-permute-start.11) | collective-permute-done | bytes 2192 | tf_op jit(solution)/shard_map/ppermute | solution.py:24
  167.5 6.9 %all-to-all-start.4 = ((f32[3,1,32,128]{3,1,0,2:T(1,128)}), f32[3,1,32,128]{3,1,0,2:T(1,128)S(1)}, u32[]{:S(2)}, u32[]{:S(2)}) async-start(f32[3,1,32,128]{3,1,0,2:T(1,128)} %copy.169), calls=%async_computation.4 | async-start | bytes 98304 | tf_op jit(solution)/shard_map/all_to_all | solution.py:114
  174.5 7.3 %all-to-all-done.4 = f32[3,1,32,128]{3,1,0,2:T(1,128)S(1)} async-done(((f32[3,1,32,128]{3,1,0,2:T(1,128)}), f32[3,1,32,128]{3,1,0,2:T(1,128)S(1)}, u32[]{:S(2)}, u32[]{:S(2)}) %all-to-all-start.4) | async-done | bytes 49184 | tf_op jit(solution)/shard_map/all_to_all | solution.py:114
  181.8 2.0 copy.171
  183.8 26.5 %scatter_custom_fusion.1 = f32[3,16384]{0,1:T(8,128)} fusion(s32[4096]{0:T(1024)} %bitcast.217, f32[4096,3]{1,0:T(8,128)} %copy.171, f32[]{:T(128)} %constant.22.clone.1), kind=kCustom, calls=%fused_computation.12 | custom fusion | flops 12288 | bytes 197120 | tf_op jit(solution)/shard_map/scatter-add | solution.py:117
  210.3 5.2 %copy.172 = f32[3,8,16,128]{3,2,1,0:T(8,128)S(1)} copy(f32[3,8,16,128]{0,3,2,1:T(8,128)} %bitcast.188) | data formatting | bytes 393216 | tf_op jit(solution)/shard_map/reshape | solution.py:126
  215.6 1.3 collective-permute-start.13
  216.9 4.6 %collective-permute-start.12 = (f32[3,1,16,128]{3,2,1,0:T(8,128)S(1)}, f32[3,1,16,128]{3,2,1,0:T(8,128)S(1)}, u32[]{:S(2)}, u32[]{:S(2)}) collective-permute-start(f32[3,1,16,128]{3,2,1,0:T(8,128)S(1)} %get-tuple-element.98), channel_id=1, source_target_pairs={{0,32},{32,64},{64,96},{96,128},{128,160},{160,192},{192,224},{1,3... | collective-permute-start | bytes 73736 | tf_op jit(solution)/shard_map/ppermute | solution.py:21
  222.4 1.3 collective-permute-start.15
  223.7 4.0 collective-permute-start.14
  228.4 4.7 %copy.174 = f32[3,8,16,128]{0,3,2,1:T(8,128)} copy(f32[3,8,16,128]{3,2,1,0:T(8,128)S(1)} %fusion.25) | data formatting | bytes 393216 | tf_op jit(solution)/shard_map/add | solution.py:125
  233.1 17.5 %gather_fusion.2 = f32[4096,3]{1,0:T(8,128)} fusion(f32[3,16384]{0,1:T(8,128)} %bitcast.193, s32[4096]{0:T(1024)S(1)} %broadcast_clamp_fusion), kind=kCustom, calls=%fused_computation.2 | custom fusion | bytes 114688 | tf_op jit(solution)/shard_map/gather | solution.py:101
  250.5 2.2 copy.175
  253.0 3.9 collective-permute-start.16
  257.6 4.3 %all-to-all-start.5 = ((f32[3,1,32,128]{3,1,0,2:T(1,128)}), f32[3,1,32,128]{3,1,0,2:T(1,128)S(1)}, u32[]{:S(2)}, u32[]{:S(2)}) async-start(f32[3,1,32,128]{3,1,0,2:T(1,128)} %broadcast_multiply_fusion.2), calls=%async_computation.5 | async-start | bytes 98304 | tf_op jit(solution)/shard_map/all_to_all | solution.py:100
  261.9 2.1 collective-permute-start.17
  264.0 1.4 maximum_maximum_fusion.2
  265.4 5.5 %collective-permute-done.17 = f32[3,10,18,1]{3,2,1,0:T(8,128)S(1)} collective-permute-done((f32[3,10,18,1]{3,2,1,0:T(8,128)S(1)}, f32[3,10,18,1]{3,2,1,0:T(8,128)S(1)}, u32[]{:S(2)}, u32[]{:S(2)}) %collective-permute-start.17) | collective-permute-done | bytes 2192 | tf_op jit(solution)/shard_map/ppermute | solution.py:24
  273.1 7.0 %all-to-all-start.6 = ((f32[3,1,32,128]{3,1,0,2:T(1,128)}), f32[3,1,32,128]{3,1,0,2:T(1,128)}, u32[]{:S(2)}, u32[]{:S(2)}) async-start(f32[3,1,32,128]{3,1,0,2:T(1,128)} %copy.177), calls=%async_computation.6 | async-start | bytes 98304 | tf_op jit(solution)/shard_map/all_to_all | solution.py:114
  280.1 7.3 %all-to-all-done.6 = f32[3,1,32,128]{3,1,0,2:T(1,128)} async-done(((f32[3,1,32,128]{3,1,0,2:T(1,128)}), f32[3,1,32,128]{3,1,0,2:T(1,128)}, u32[]{:S(2)}, u32[]{:S(2)}) %all-to-all-start.6) | async-done | bytes 49184 | tf_op jit(solution)/shard_map/all_to_all | solution.py:114
  288.3 2.0 copy.179
  290.3 26.5 %scatter_custom_fusion.2 = f32[3,16384]{0,1:T(8,128)} fusion(s32[4096]{0:T(1024)} %bitcast.218, f32[4096,3]{1,0:T(8,128)} %copy.179, f32[]{:T(128)} %constant.22.clone.1), kind=kCustom, calls=%fused_computation.10 | custom fusion | flops 12288 | bytes 197120 | tf_op jit(solution)/shard_map/scatter-add | solution.py:117
  316.7 5.2 %copy.180 = f32[3,8,16,128]{3,2,1,0:T(8,128)S(1)} copy(f32[3,8,16,128]{0,3,2,1:T(8,128)} %bitcast.189) | data formatting | bytes 393216 | tf_op jit(solution)/shard_map/reshape | solution.py:126
  322.0 1.3 collective-permute-start.19
  323.3 4.9 %collective-permute-start.18 = (f32[3,1,16,128]{3,2,1,0:T(8,128)S(1)}, f32[3,1,16,128]{3,2,1,0:T(8,128)S(1)}, u32[]{:S(2)}, u32[]{:S(2)}) collective-permute-start(f32[3,1,16,128]{3,2,1,0:T(8,128)S(1)} %get-tuple-element.93), channel_id=1, source_target_pairs={{0,32},{32,64},{64,96},{96,128},{128,160},{160,192},{192,224},{1,3... | collective-permute-start | bytes 73736 | tf_op jit(solution)/shard_map/ppermute | solution.py:21
  329.2 1.3 collective-permute-start.21
  330.5 4.2 collective-permute-start.20
  334.7 4.7 %copy.182 = f32[3,8,16,128]{0,3,2,1:T(8,128)} copy(f32[3,8,16,128]{3,2,1,0:T(8,128)S(1)} %fusion.28) | data formatting | bytes 393216 | tf_op jit(solution)/shard_map/add | solution.py:125
  339.4 17.5 %gather_fusion.3 = f32[4096,3]{1,0:T(8,128)} fusion(f32[3,16384]{0,1:T(8,128)} %bitcast.191, s32[4096]{0:T(1024)S(1)} %broadcast_clamp_fusion), kind=kCustom, calls=%fused_computation.3 | custom fusion | bytes 114688 | tf_op jit(solution)/shard_map/gather | solution.py:101
  356.9 2.2 copy.183
  360.1 3.9 collective-permute-start.22
  364.6 4.3 %all-to-all-start.7 = ((f32[3,1,32,128]{3,1,0,2:T(1,128)}), f32[3,1,32,128]{3,1,0,2:T(1,128)S(1)}, u32[]{:S(2)}, u32[]{:S(2)}) async-start(f32[3,1,32,128]{3,1,0,2:T(1,128)} %broadcast_multiply_fusion.1), calls=%async_computation.7 | async-start | bytes 98304 | tf_op jit(solution)/shard_map/all_to_all | solution.py:100
  369.0 2.1 collective-permute-start.23
  371.1 1.4 maximum_maximum_fusion.3
  372.5 5.5 %collective-permute-done.23 = f32[3,10,18,1]{3,2,1,0:T(8,128)S(1)} collective-permute-done((f32[3,10,18,1]{3,2,1,0:T(8,128)S(1)}, f32[3,10,18,1]{3,2,1,0:T(8,128)S(1)}, u32[]{:S(2)}, u32[]{:S(2)}) %collective-permute-start.23) | collective-permute-done | bytes 2192 | tf_op jit(solution)/shard_map/ppermute | solution.py:24
  380.4 6.9 %all-to-all-start.8 = ((f32[3,1,32,128]{3,1,0,2:T(1,128)}), f32[3,1,32,128]{3,1,0,2:T(1,128)S(1)}, u32[]{:S(2)}, u32[]{:S(2)}) async-start(f32[3,1,32,128]{3,1,0,2:T(1,128)} %copy.185), calls=%async_computation.8 | async-start | bytes 98304 | tf_op jit(solution)/shard_map/all_to_all | solution.py:114
  388.6 6.0 %all-to-all-done.8 = f32[3,1,32,128]{3,1,0,2:T(1,128)S(1)} async-done(((f32[3,1,32,128]{3,1,0,2:T(1,128)}), f32[3,1,32,128]{3,1,0,2:T(1,128)S(1)}, u32[]{:S(2)}, u32[]{:S(2)}) %all-to-all-start.8) | async-done | bytes 49184 | tf_op jit(solution)/shard_map/all_to_all | solution.py:114
  395.4 26.3 %scatter_custom_fusion.3 = f32[3,16384]{0,1:T(8,128)} fusion(s32[4096]{0:T(1024)} %bitcast.219, f32[4096,3]{1,0:T(8,128)S(1)} %copy.187, f32[]{:T(128)} %constant.22.clone.1), kind=kCustom, calls=%fused_computation.8 | custom fusion | flops 12288 | bytes 197120 | tf_op jit(solution)/shard_map/scatter-add | solution.py:117
  421.7 5.2 %copy.188 = f32[3,8,16,128]{3,2,1,0:T(8,128)S(1)} copy(f32[3,8,16,128]{0,3,2,1:T(8,128)} %bitcast.186) | data formatting | bytes 393216 | tf_op jit(solution)/shard_map/reshape | solution.py:126
  (166 shorter events, 27.8 us)
Async XLA Ops:
  0.6 23.2 %copy-start = (f32[3,8,16,128]{3,2,1,0:T(8,128)S(1)}, f32[3,8,16,128]{3,2,1,0:T(8,128)}, u32[]{:S(2)}) copy-start(f32[3,8,16,128]{3,2,1,0:T(8,128)} %param.9) | copy-start | bytes 589828
  0.6 22.6 %all-to-all-start = ((s32[1,32,128]{2,0,1:T(1,128)}), s32[1,32,128]{2,0,1:T(1,128)S(1)}, u32[]{:S(2)}, u32[]{:S(2)}) async-start(s32[1,32,128]{2,0,1:T(1,128)} %bitcast.220), calls=%async_computation | async-start | bytes 32768 | tf_op jit(solution)/shard_map/all_to_all | solution.py:75
  10.1 13.7 %collective-permute-start = (f32[3,1,16,128]{3,2,1,0:T(8,128)S(1)}, f32[3,1,16,128]{3,2,1,0:T(8,128)S(1)}, u32[]{:S(2)}, u32[]{:S(2)}) collective-permute-start(f32[3,1,16,128]{3,2,1,0:T(8,128)S(1)} %get-tuple-element.109), channel_id=1, source_target_pairs={{0,32},{32,64},{64,96},{96,128},{128,160},{160,192},{192,224},{1,3... | collective-permute-start | bytes 73736 | tf_op jit(solution)/shard_map/ppermute | solution.py:21
  13.7 10.2 %collective-permute-start.1 = (f32[3,1,16,128]{3,2,1,0:T(8,128)S(1)}, f32[3,1,16,128]{3,2,1,0:T(8,128)S(1)}, u32[]{:S(2)}, u32[]{:S(2)}) collective-permute-start(f32[3,1,16,128]{3,2,1,0:T(8,128)S(1)} %get-tuple-element.108), channel_id=1, source_target_pairs={{32,0},{64,32},{96,64},{128,96},{160,128},{192,160},{224,192},{33,... | collective-permute-start | bytes 73736 | tf_op jit(solution)/shard_map/ppermute | solution.py:24
  23.2 42.5 %copy-start.8 = (f32[2,3,1,32,128]{4,3,2,1,0:T(8,128)S(1)}, f32[2,3,1,32,128]{4,3,2,1,0:T(8,128)}, u32[]{:S(2)}) copy-start(f32[2,3,1,32,128]{4,3,2,1,0:T(8,128)} %param.12) | copy-start | bytes 294916
  24.0 20.1 %collective-permute-start.3 = (f32[3,10,1,128]{3,2,1,0:T(1,128)S(1)}, f32[3,10,1,128]{3,2,1,0:T(1,128)S(1)}, u32[]{:S(2)}, u32[]{:S(2)}) collective-permute-start(f32[3,10,1,128]{3,2,1,0:T(1,128)S(1)} %get-tuple-element.89), channel_id=1, source_target_pairs={{8,0},{16,8},{24,16},{9,1},{17,9},{25,17},{10,2},{18,10},{26,18},{... | collective-permute-start | bytes 46088 | tf_op jit(solution)/shard_map/ppermute | solution.py:24
  25.3 18.8 %collective-permute-start.2 = (f32[3,10,1,128]{3,2,1,0:T(1,128)S(1)}, f32[3,10,1,128]{3,2,1,0:T(1,128)S(1)}, u32[]{:S(2)}, u32[]{:S(2)}) collective-permute-start(f32[3,10,1,128]{3,2,1,0:T(1,128)S(1)} %get-tuple-element.88), channel_id=1, source_target_pairs={{0,8},{8,16},{16,24},{1,9},{9,17},{17,25},{2,10},{10,18},{18,26},{... | collective-permute-start | bytes 46088 | tf_op jit(solution)/shard_map/ppermute | solution.py:21
  29.3 36.4 %copy-start.3 = (f32[1,32,128]{2,0,1:T(1,128)}, f32[1,32,128]{2,0,1:T(1,128)S(1)}, u32[]{:S(2)}) copy-start(f32[1,32,128]{2,0,1:T(1,128)S(1)} %compare_convert_fusion) | copy-start | bytes 49156
  44.3 13.9 %collective-permute-start.4 = (f32[3,10,18,1]{3,2,1,0:T(8,128)S(1)}, f32[3,10,18,1]{3,2,1,0:T(8,128)S(1)}, u32[]{:S(2)}, u32[]{:S(2)}) collective-permute-start(f32[3,10,18,1]{3,2,1,0:T(8,128)S(1)} %get-tuple-element.81), channel_id=1, source_target_pairs={{0,1},{1,2},{2,3},{3,4},{4,5},{5,6},{6,7},{8,9},{9,10},{10,11},{11... | collective-permute-start | bytes 6488 | tf_op jit(solution)/shard_map/ppermute | solution.py:21
  49.4 16.3 %all-to-all-start.1 = ((f32[3,1,32,128]{3,1,0,2:T(1,128)}), f32[3,1,32,128]{3,1,0,2:T(1,128)S(1)}, u32[]{:S(2)}, u32[]{:S(2)}) async-start(f32[3,1,32,128]{3,1,0,2:T(1,128)} %broadcast_multiply_fusion.4), calls=%async_computation.1 | async-start | bytes 98304 | tf_op jit(solution)/shard_map/all_to_all | solution.py:100
  56.0 9.0 %collective-permute-start.5 = (f32[3,10,18,1]{3,2,1,0:T(8,128)S(1)}, f32[3,10,18,1]{3,2,1,0:T(8,128)S(1)}, u32[]{:S(2)}, u32[]{:S(2)}) collective-permute-start(f32[3,10,18,1]{3,2,1,0:T(8,128)S(1)} %get-tuple-element.80), channel_id=1, source_target_pairs={{1,0},{2,1},{3,2},{4,3},{5,4},{6,5},{7,6},{9,8},{10,9},{11,10},{12... | collective-permute-start | bytes 6488 | tf_op jit(solution)/shard_map/ppermute | solution.py:24
  67.0 14.3 %all-to-all-start.2 = ((f32[3,1,32,128]{3,1,0,2:T(1,128)}), f32[3,1,32,128]{3,1,0,2:T(1,128)S(1)}, u32[]{:S(2)}, u32[]{:S(2)}) async-start(f32[3,1,32,128]{3,1,0,2:T(1,128)} %copy.161), calls=%async_computation.2 | async-start | bytes 98304 | tf_op jit(solution)/shard_map/all_to_all | solution.py:114
  82.0 31.7 %copy-start.1 = (f32[3,8,16,128]{3,2,1,0:T(8,128)S(1)}, f32[3,8,16,128]{3,2,1,0:T(8,128)}, u32[]{:S(2)}) copy-start(f32[3,8,16,128]{3,2,1,0:T(8,128)} %param.9) | copy-start | bytes 589828
  108.3 5.4 %copy-start.13 = (f32[1,8,16,128]{3,2,1,0:T(8,128)S(1)}, f32[1,8,16,128]{3,2,1,0:T(8,128)}, u32[]{:S(2)}) copy-start(f32[1,8,16,128]{3,2,1,0:T(8,128)} %get-tuple-element.105) | copy-start | bytes 196612
  108.3 5.4 %copy-start.14 = (f32[1,8,16,128]{3,2,1,0:T(8,128)S(1)}, f32[1,8,16,128]{3,2,1,0:T(8,128)}, u32[]{:S(2)}) copy-start(f32[1,8,16,128]{3,2,1,0:T(8,128)} %get-tuple-element.106) | copy-start | bytes 196612
  108.3 5.4 %copy-start.15 = (f32[1,8,16,128]{3,2,1,0:T(8,128)S(1)}, f32[1,8,16,128]{3,2,1,0:T(8,128)}, u32[]{:S(2)}) copy-start(f32[1,8,16,128]{3,2,1,0:T(8,128)} %get-tuple-element.107) | copy-start | bytes 196612
  108.3 17.9 %copy-start.5 = (f32[1,32,128]{2,1,0:T(8,128)S(1)}, f32[1,32,128]{2,1,0:T(8,128)}, u32[]{:S(2)}) copy-start(f32[1,32,128]{2,1,0:T(8,128)} %param.14) | copy-start | bytes 49156
  108.3 18.0 %copy-start.9 = (f32[1,32,128]{2,1,0:T(8,128)S(1)}, f32[1,32,128]{2,1,0:T(8,128)}, u32[]{:S(2)}) copy-start(f32[1,32,128]{2,1,0:T(8,128)} %param.16) | copy-start | bytes 49156
  108.3 18.0 %copy-start.16 = (f32[1,32,128]{2,1,0:T(8,128)S(1)}, f32[1,32,128]{2,1,0:T(8,128)}, u32[]{:S(2)}) copy-start(f32[1,32,128]{2,1,0:T(8,128)} %param.17) | copy-start | bytes 49156
  108.3 17.9 %copy-start.18 = (f32[2,1,32,128]{3,2,1,0:T(8,128)S(1)}, f32[2,1,32,128]{3,2,1,0:T(8,128)}, u32[]{:S(2)}) copy-start(f32[2,1,32,128]{3,2,1,0:T(8,128)} %param.13) | copy-start | bytes 98308
  108.3 17.9 %copy-start.21 = (f32[32,128]{1,0:T(8,128)S(1)}, f32[32,128]{1,0:T(8,128)}, u32[]{:S(2)}) copy-start(f32[32,128]{1,0:T(8,128)} %get-tuple-element.37) | copy-start | bytes 49156
  113.8 6.2 %collective-permute-start.7 = (f32[3,1,16,128]{3,2,1,0:T(8,128)S(1)}, f32[3,1,16,128]{3,2,1,0:T(8,128)S(1)}, u32[]{:S(2)}, u32[]{:S(2)}) collective-permute-start(f32[3,1,16,128]{3,2,1,0:T(8,128)S(1)} %get-tuple-element.104), channel_id=1, source_target_pairs={{32,0},{64,32},{96,64},{128,96},{160,128},{192,160},{224,192},{33,... | collective-permute-start | bytes 73736 | tf_op jit(solution)/shard_map/ppermute | solution.py:24
  115.1 5.8 %collective-permute-start.6 = (f32[3,1,16,128]{3,2,1,0:T(8,128)S(1)}, f32[3,1,16,128]{3,2,1,0:T(8,128)S(1)}, u32[]{:S(2)}, u32[]{:S(2)}) collective-permute-start(f32[3,1,16,128]{3,2,1,0:T(8,128)S(1)} %get-tuple-element.103), channel_id=1, source_target_pairs={{0,32},{32,64},{64,96},{96,128},{128,160},{160,192},{192,224},{1,3... | collective-permute-start | bytes 73736 | tf_op jit(solution)/shard_map/ppermute | solution.py:21
  121.0 25.4 %collective-permute-start.9 = (f32[3,10,1,128]{3,2,1,0:T(1,128)S(1)}, f32[3,10,1,128]{3,2,1,0:T(1,128)S(1)}, u32[]{:S(2)}, u32[]{:S(2)}) collective-permute-start(f32[3,10,1,128]{3,2,1,0:T(1,128)S(1)} %get-tuple-element.87), channel_id=1, source_target_pairs={{8,0},{16,8},{24,16},{9,1},{17,9},{25,17},{10,2},{18,10},{26,18},{... | collective-permute-start | bytes 46088 | tf_op jit(solution)/shard_map/ppermute | solution.py:24
  122.3 24.1 %collective-permute-start.8 = (f32[3,10,1,128]{3,2,1,0:T(1,128)S(1)}, f32[3,10,1,128]{3,2,1,0:T(1,128)S(1)}, u32[]{:S(2)}, u32[]{:S(2)}) collective-permute-start(f32[3,10,1,128]{3,2,1,0:T(1,128)S(1)} %get-tuple-element.86), channel_id=1, source_target_pairs={{0,8},{8,16},{16,24},{1,9},{9,17},{17,25},{2,10},{10,18},{18,26},{... | collective-permute-start | bytes 46088 | tf_op jit(solution)/shard_map/ppermute | solution.py:21
  146.6 11.7 %collective-permute-start.10 = (f32[3,10,18,1]{3,2,1,0:T(8,128)S(1)}, f32[3,10,18,1]{3,2,1,0:T(8,128)S(1)}, u32[]{:S(2)}, u32[]{:S(2)}) collective-permute-start(f32[3,10,18,1]{3,2,1,0:T(8,128)S(1)} %get-tuple-element.79), channel_id=1, source_target_pairs={{0,1},{1,2},{2,3},{3,4},{4,5},{5,6},{6,7},{8,9},{9,10},{10,11},{11... | collective-permute-start | bytes 6488 | tf_op jit(solution)/shard_map/ppermute | solution.py:21
  151.9 14.1 %all-to-all-start.3 = ((f32[3,1,32,128]{3,1,0,2:T(1,128)}), f32[3,1,32,128]{3,1,0,2:T(1,128)S(1)}, u32[]{:S(2)}, u32[]{:S(2)}) async-start(f32[3,1,32,128]{3,1,0,2:T(1,128)} %broadcast_multiply_fusion.3), calls=%async_computation.3 | async-start | bytes 98304 | tf_op jit(solution)/shard_map/all_to_all | solution.py:100
  156.2 9.0 %collective-permute-start.11 = (f32[3,10,18,1]{3,2,1,0:T(8,128)S(1)}, f32[3,10,18,1]{3,2,1,0:T(8,128)S(1)}, u32[]{:S(2)}, u32[]{:S(2)}) collective-permute-start(f32[3,10,18,1]{3,2,1,0:T(8,128)S(1)} %get-tuple-element.78), channel_id=1, source_target_pairs={{1,0},{2,1},{3,2},{4,3},{5,4},{6,5},{7,6},{9,8},{10,9},{11,10},{12... | collective-permute-start | bytes 6488 | tf_op jit(solution)/shard_map/ppermute | solution.py:24
  167.5 14.3 %all-to-all-start.4 = ((f32[3,1,32,128]{3,1,0,2:T(1,128)}), f32[3,1,32,128]{3,1,0,2:T(1,128)S(1)}, u32[]{:S(2)}, u32[]{:S(2)}) async-start(f32[3,1,32,128]{3,1,0,2:T(1,128)} %copy.169), calls=%async_computation.4 | async-start | bytes 98304 | tf_op jit(solution)/shard_map/all_to_all | solution.py:114
  183.8 43.9 %copy-start.6 = (f32[1,32,128]{2,1,0:T(8,128)S(1)}, f32[1,32,128]{2,1,0:T(8,128)}, u32[]{:S(2)}) copy-start(f32[1,32,128]{2,1,0:T(8,128)} %param.14) | copy-start | bytes 49156
  183.8 43.9 %copy-start.10 = (f32[1,32,128]{2,1,0:T(8,128)S(1)}, f32[1,32,128]{2,1,0:T(8,128)}, u32[]{:S(2)}) copy-start(f32[1,32,128]{2,1,0:T(8,128)} %param.16) | copy-start | bytes 49156
  183.8 43.9 %copy-start.17 = (f32[1,32,128]{2,1,0:T(8,128)S(1)}, f32[1,32,128]{2,1,0:T(8,128)}, u32[]{:S(2)}) copy-start(f32[1,32,128]{2,1,0:T(8,128)} %param.17) | copy-start | bytes 49156
  183.8 43.9 %copy-start.19 = (f32[1,32,128]{2,1,0:T(8,128)S(1)}, f32[1,32,128]{2,1,0:T(8,128)}, u32[]{:S(2)}) copy-start(f32[1,32,128]{2,1,0:T(8,128)} %get-tuple-element.35) | copy-start | bytes 49156
  183.8 43.9 %copy-start.20 = (f32[1,32,128]{2,1,0:T(8,128)S(1)}, f32[1,32,128]{2,1,0:T(8,128)}, u32[]{:S(2)}) copy-start(f32[1,32,128]{2,1,0:T(8,128)} %get-tuple-element.36) | copy-start | bytes 49156
  215.5 41.4 %copy-start.4 = (f32[1,32,128]{2,0,1:T(1,128)S(1)}, f32[1,32,128]{2,0,1:T(1,128)}, u32[]{:S(2)}) copy-start(f32[1,32,128]{2,0,1:T(1,128)} %copy-done.3) | copy-start | bytes 49156
  215.6 5.9 %collective-permute-start.13 = (f32[3,1,16,128]{3,2,1,0:T(8,128)S(1)}, f32[3,1,16,128]{3,2,1,0:T(8,128)S(1)}, u32[]{:S(2)}, u32[]{:S(2)}) collective-permute-start(f32[3,1,16,128]{3,2,1,0:T(8,128)S(1)} %get-tuple-element.99), channel_id=1, source_target_pairs={{32,0},{64,32},{96,64},{128,96},{160,128},{192,160},{224,192},{33,... | collective-permute-start | bytes 73736 | tf_op jit(solution)/shard_map/ppermute | solution.py:24
  216.9 5.5 %collective-permute-start.12 = (f32[3,1,16,128]{3,2,1,0:T(8,128)S(1)}, f32[3,1,16,128]{3,2,1,0:T(8,128)S(1)}, u32[]{:S(2)}, u32[]{:S(2)}) collective-permute-start(f32[3,1,16,128]{3,2,1,0:T(8,128)S(1)} %get-tuple-element.98), channel_id=1, source_target_pairs={{0,32},{32,64},{64,96},{96,128},{128,160},{160,192},{192,224},{1,3... | collective-permute-start | bytes 73736 | tf_op jit(solution)/shard_map/ppermute | solution.py:21
  222.4 30.3 %collective-permute-start.15 = (f32[3,10,1,128]{3,2,1,0:T(1,128)S(1)}, f32[3,10,1,128]{3,2,1,0:T(1,128)S(1)}, u32[]{:S(2)}, u32[]{:S(2)}) collective-permute-start(f32[3,10,1,128]{3,2,1,0:T(1,128)S(1)} %get-tuple-element.85), channel_id=1, source_target_pairs={{8,0},{16,8},{24,16},{9,1},{17,9},{25,17},{10,2},{18,10},{26,18},{... | collective-permute-start | bytes 46088 | tf_op jit(solution)/shard_map/ppermute | solution.py:24
  223.7 29.0 %collective-permute-start.14 = (f32[3,10,1,128]{3,2,1,0:T(1,128)S(1)}, f32[3,10,1,128]{3,2,1,0:T(1,128)S(1)}, u32[]{:S(2)}, u32[]{:S(2)}) collective-permute-start(f32[3,10,1,128]{3,2,1,0:T(1,128)S(1)} %get-tuple-element.84), channel_id=1, source_target_pairs={{0,8},{8,16},{16,24},{1,9},{9,17},{17,25},{2,10},{10,18},{18,26},{... | collective-permute-start | bytes 46088 | tf_op jit(solution)/shard_map/ppermute | solution.py:21
  253.0 11.0 %collective-permute-start.16 = (f32[3,10,18,1]{3,2,1,0:T(8,128)S(1)}, f32[3,10,18,1]{3,2,1,0:T(8,128)}, u32[]{:S(2)}, u32[]{:S(2)}) collective-permute-start(f32[3,10,18,1]{3,2,1,0:T(8,128)S(1)} %get-tuple-element.77), channel_id=1, source_target_pairs={{0,1},{1,2},{2,3},{3,4},{4,5},{5,6},{6,7},{8,9},{9,10},{10,11},{11... | collective-permute-start | bytes 6488 | tf_op jit(solution)/shard_map/ppermute | solution.py:21
  257.6 14.2 %all-to-all-start.5 = ((f32[3,1,32,128]{3,1,0,2:T(1,128)}), f32[3,1,32,128]{3,1,0,2:T(1,128)S(1)}, u32[]{:S(2)}, u32[]{:S(2)}) async-start(f32[3,1,32,128]{3,1,0,2:T(1,128)} %broadcast_multiply_fusion.2), calls=%async_computation.5 | async-start | bytes 98304 | tf_op jit(solution)/shard_map/all_to_all | solution.py:100
  261.9 9.0 %collective-permute-start.17 = (f32[3,10,18,1]{3,2,1,0:T(8,128)S(1)}, f32[3,10,18,1]{3,2,1,0:T(8,128)S(1)}, u32[]{:S(2)}, u32[]{:S(2)}) collective-permute-start(f32[3,10,18,1]{3,2,1,0:T(8,128)S(1)} %get-tuple-element.76), channel_id=1, source_target_pairs={{1,0},{2,1},{3,2},{4,3},{5,4},{6,5},{7,6},{9,8},{10,9},{11,10},{12... | collective-permute-start | bytes 6488 | tf_op jit(solution)/shard_map/ppermute | solution.py:24
  273.1 14.4 %all-to-all-start.6 = ((f32[3,1,32,128]{3,1,0,2:T(1,128)}), f32[3,1,32,128]{3,1,0,2:T(1,128)}, u32[]{:S(2)}, u32[]{:S(2)}) async-start(f32[3,1,32,128]{3,1,0,2:T(1,128)} %copy.177), calls=%async_computation.6 | async-start | bytes 98304 | tf_op jit(solution)/shard_map/all_to_all | solution.py:114
  290.3 38.0 %copy-start.22 = (f32[1,32,128]{2,1,0:T(8,128)S(1)}, f32[1,32,128]{2,1,0:T(8,128)}, u32[]{:S(2)}) copy-start(f32[1,32,128]{2,1,0:T(8,128)} %get-tuple-element.30) | copy-start | bytes 49156
  290.3 38.0 %copy-start.23 = (f32[1,32,128]{2,1,0:T(8,128)S(1)}, f32[1,32,128]{2,1,0:T(8,128)}, u32[]{:S(2)}) copy-start(f32[1,32,128]{2,1,0:T(8,128)} %get-tuple-element.31) | copy-start | bytes 49156
  290.3 38.0 %copy-start.24 = (f32[32,128]{1,0:T(8,128)S(1)}, f32[32,128]{1,0:T(8,128)}, u32[]{:S(2)}) copy-start(f32[32,128]{1,0:T(8,128)} %get-tuple-element.27) | copy-start | bytes 49156
  322.0 6.3 %collective-permute-start.19 = (f32[3,1,16,128]{3,2,1,0:T(8,128)S(1)}, f32[3,1,16,128]{3,2,1,0:T(8,128)S(1)}, u32[]{:S(2)}, u32[]{:S(2)}) collective-permute-start(f32[3,1,16,128]{3,2,1,0:T(8,128)S(1)} %get-tuple-element.94), channel_id=1, source_target_pairs={{32,0},{64,32},{96,64},{128,96},{160,128},{192,160},{224,192},{33,... | collective-permute-start | bytes 73736 | tf_op jit(solution)/shard_map/ppermute | solution.py:24
  323.3 5.8 %collective-permute-start.18 = (f32[3,1,16,128]{3,2,1,0:T(8,128)S(1)}, f32[3,1,16,128]{3,2,1,0:T(8,128)S(1)}, u32[]{:S(2)}, u32[]{:S(2)}) collective-permute-start(f32[3,1,16,128]{3,2,1,0:T(8,128)S(1)} %get-tuple-element.93), channel_id=1, source_target_pairs={{0,32},{32,64},{64,96},{96,128},{128,160},{160,192},{192,224},{1,3... | collective-permute-start | bytes 73736 | tf_op jit(solution)/shard_map/ppermute | solution.py:21
  329.2 29.9 %collective-permute-start.21 = (f32[3,10,1,128]{3,2,1,0:T(1,128)S(1)}, f32[3,10,1,128]{3,2,1,0:T(1,128)S(1)}, u32[]{:S(2)}, u32[]{:S(2)}) collective-permute-start(f32[3,10,1,128]{3,2,1,0:T(1,128)S(1)} %get-tuple-element.83), channel_id=1, source_target_pairs={{8,0},{16,8},{24,16},{9,1},{17,9},{25,17},{10,2},{18,10},{26,18},{... | collective-permute-start | bytes 46088 | tf_op jit(solution)/shard_map/ppermute | solution.py:24
  330.5 28.6 %collective-permute-start.20 = (f32[3,10,1,128]{3,2,1,0:T(1,128)S(1)}, f32[3,10,1,128]{3,2,1,0:T(1,128)S(1)}, u32[]{:S(2)}, u32[]{:S(2)}) collective-permute-start(f32[3,10,1,128]{3,2,1,0:T(1,128)S(1)} %get-tuple-element.82), channel_id=1, source_target_pairs={{0,8},{8,16},{16,24},{1,9},{9,17},{17,25},{2,10},{10,18},{18,26},{... | collective-permute-start | bytes 46088 | tf_op jit(solution)/shard_map/ppermute | solution.py:21
  359.1 28.2 %copy-start.7 = (f32[1,32,128]{2,1,0:T(8,128)S(1)}, f32[1,32,128]{2,1,0:T(8,128)}, u32[]{:S(2)}) copy-start(f32[1,32,128]{2,1,0:T(8,128)} %param.14) | copy-start | bytes 49156
  360.1 11.0 %collective-permute-start.22 = (f32[3,10,18,1]{3,2,1,0:T(8,128)}, f32[3,10,18,1]{3,2,1,0:T(8,128)}, u32[]{:S(2)}, u32[]{:S(2)}) collective-permute-start(f32[3,10,18,1]{3,2,1,0:T(8,128)} %get-tuple-element.75), channel_id=1, source_target_pairs={{0,1},{1,2},{2,3},{3,4},{4,5},{5,6},{6,7},{8,9},{9,10},{10,11},{11... | collective-permute-start | bytes 6488 | tf_op jit(solution)/shard_map/ppermute | solution.py:21
  364.6 15.0 %all-to-all-start.7 = ((f32[3,1,32,128]{3,1,0,2:T(1,128)}), f32[3,1,32,128]{3,1,0,2:T(1,128)S(1)}, u32[]{:S(2)}, u32[]{:S(2)}) async-start(f32[3,1,32,128]{3,1,0,2:T(1,128)} %broadcast_multiply_fusion.1), calls=%async_computation.7 | async-start | bytes 98304 | tf_op jit(solution)/shard_map/all_to_all | solution.py:100
  369.0 9.0 %collective-permute-start.23 = (f32[3,10,18,1]{3,2,1,0:T(8,128)S(1)}, f32[3,10,18,1]{3,2,1,0:T(8,128)S(1)}, u32[]{:S(2)}, u32[]{:S(2)}) collective-permute-start(f32[3,10,18,1]{3,2,1,0:T(8,128)S(1)} %get-tuple-element.74), channel_id=1, source_target_pairs={{1,0},{2,1},{3,2},{4,3},{5,4},{6,5},{7,6},{9,8},{10,9},{11,10},{12... | collective-permute-start | bytes 6488 | tf_op jit(solution)/shard_map/ppermute | solution.py:24
  378.8 48.1 %copy-start.2 = (f32[3,8,16,128]{3,2,1,0:T(8,128)}, f32[3,8,16,128]{3,2,1,0:T(8,128)S(1)}, u32[]{:S(2)}) copy-start(f32[3,8,16,128]{3,2,1,0:T(8,128)S(1)} %get-tuple-element.26) | copy-start | bytes 589828
  380.4 14.3 %all-to-all-start.8 = ((f32[3,1,32,128]{3,1,0,2:T(1,128)}), f32[3,1,32,128]{3,1,0,2:T(1,128)S(1)}, u32[]{:S(2)}, u32[]{:S(2)}) async-start(f32[3,1,32,128]{3,1,0,2:T(1,128)} %copy.185), calls=%async_computation.8 | async-start | bytes 98304 | tf_op jit(solution)/shard_map/all_to_all | solution.py:114
  395.3 31.5 %copy-start.11 = (f32[1,8,16,128]{3,2,1,0:T(8,128)S(1)}, f32[1,8,16,128]{3,2,1,0:T(8,128)}, u32[]{:S(2)}) copy-start(f32[1,8,16,128]{3,2,1,0:T(8,128)} %get-tuple-element.91) | copy-start | bytes 196612
  395.4 31.5 %copy-start.12 = (f32[1,8,16,128]{3,2,1,0:T(8,128)S(1)}, f32[1,8,16,128]{3,2,1,0:T(8,128)}, u32[]{:S(2)}) copy-start(f32[1,8,16,128]{3,2,1,0:T(8,128)} %get-tuple-element.92) | copy-start | bytes 196612
where the time goes:
time: 434 us; the launch traced here: 428 us
  other arithmetic  126 us (29%)
  starting transfers between devices  125 us (29%)
  local copies, waits for them, and re-layouts  121 us (28%)
  waiting for transfers between devices  53.8 us (12%)
    scatter-add x4, other arithmetic, shards(): jnp.zeros((3, cell_count), jnp.float32).at[:, dropped]  106 us
    gather x8, local copies, waits for them, and re-layouts, shards(): electric.reshape(3, -1)[:, safe_index] * weight  68.9 us
    ppermute x12, starting transfers between devices, extended_2(): lax.ppermute(lax.slice_in_dim(block, block.shape[dim] - width, None, axis...  50.1 us
    all_to_all x4, starting transfers between devices, shards(): lax.all_to_all(change, ('gy', 'gz'), split_axis=2, concat_axis=2, tiled=T...  27.8 us
    all_to_all x4, waiting for transfers between devices, shards(): lax.all_to_all(change, ('gy', 'gz'), split_axis=2, concat_axis=2, tiled=T...  27.3 us
    ppermute x12, waiting for transfers between devices, extended_2(): lax.ppermute(lax.slice_in_dim(block, 0, width, axis=dim), axis, backward)  23.8 us
    reshape x4, local copies, waits for them, and re-layouts, shards(): summed.reshape(3, width_x, width_y, width_z)  21 us
    all_to_all x4, starting transfers between devices, shards(): lax.all_to_all((electric.reshape(3, -1)[:, safe_index] * weight).reshape(...  19.6 us
  transfers between devices with their start and end apart: 33, of which 11 were waited for; matrix products, arithmetic and copies ran while one was open for 25% of the time, Pallas kernels for 0%

commit v1 on v0

v1 whole, which is shorter than its diff:
```python
import functools

import jax
import jax.numpy as jnp
from jax import lax
from jax.experimental import pallas as pl
from jax.experimental.pallas import tpu as pltpu
from jax.sharding import PartitionSpec as P

MESH = pl.DeviceIdType.MESH
STEPS = 4
DT = 0.5
PUMP_DECAY = 0.2
UPPER_DECAY = 0.02
WORK_SHARE = 0.05
EPSILON = (1.0, 2.1, 6.0, 12.25)
F32 = jnp.float32
BF16 = jnp.bfloat16
LANES = 128
ROWS = 128
HALF = 64
CY = 16
CX = 8


def split(x):
    hi = x.astype(BF16)
    return hi, (x - hi.astype(F32)).astype(BF16)


def kernel(
    sizes,
    e_in,
    cls_in,
    idx_in,
    pol_in,
    pop_in,
    res_in,
    dep_in,
    cou_in,
    pum_in,
    e_out,
    h_out,
    pol_out,
    pop_out,
    ef,
    hf,
    inv,
    cls,
    own,
    oidx,
    st,
    sidx,
    back,
    ret,
    coef,
    qsel,
    wide,
    tall,
    pick,
    el,
    amat,
    samp,
    ey_s,
    ez_s,
    hy_s,
    hz_s,
    ex_r,
    ey_r,
    ez_r,
    hx_r,
    hy_r,
    hz_r,
    load_sem,
    self_sem,
    idx_ss,
    idx_rs,
    st_ss,
    st_rs,
    b0_ss,
    b0_rs,
    b1_ss,
    b1_rs,
    eh_ss,
    eh_rs,
    hh_ss,
    hh_rs,
    out_sem,
):
    n_gx, n_gy, n_gz = sizes
    group = n_gy * n_gz
    ax = lax.axis_index("gx")
    ay = lax.axis_index("gy")
    az = lax.axis_index("gz")
    me = ay * n_gz + az
    down = (
        (lax.rem(ax + n_gx - 1, n_gx), ay, az),
        (ax, lax.rem(ay + n_gy - 1, n_gy), az),
        (ax, ay, lax.rem(az + n_gz - 1, n_gz)),
    )
    up = (
        (lax.rem(ax + 1, n_gx), ay, az),
        (ax, lax.rem(ay + 1, n_gy), az),
        (ax, ay, lax.rem(az + 1, n_gz)),
    )

    def peer(p):
        return (ax, p // n_gz, lax.rem(p, n_gz))

    loads = (
        (idx_in, oidx),
        (e_in, ef),
        (cls_in, cls),
        (pol_in, own.at[pl.ds(0, 6)]),
        (pop_in, own.at[pl.ds(6, 2)]),
        (res_in, own.at[8]),
        (dep_in, own.at[9]),
        (cou_in, own.at[10]),
        (pum_in, own.at[11]),
    )
    loads = [
        pltpu.make_async_copy(src, dst, load_sem.at[i])
        for i, (src, dst) in enumerate(loads)
    ]
    for copy in loads:
        copy.start()

    barrier = pltpu.get_barrier_semaphore()

    def greet(o, carry):
        pl.semaphore_signal(
            barrier, inc=1, device_id=peer(lax.rem(me + o, group)), device_id_type=MESH
        )
        return carry

    lax.fori_loop(1, group, greet, 0)
    greetings = group - 1
    if n_gx > 1:
        for other in (down[0], up[0]):
            pl.semaphore_signal(barrier, inc=1, device_id=other, device_id_type=MESH)
        greetings += 2

    for copy in loads:
        copy.wait()

    def row(buf, p):
        if len(buf.shape) == 2:
            return buf.at[pl.ds(p, 1), :]
        return buf.at[:, pl.ds(p, 1), :]

    def exchange(src, dst, ss, rs, sem):
        def there(o):
            p = lax.rem(me + o, group)
            return pltpu.make_async_remote_copy(
                src_ref=row(src, p),
                dst_ref=row(dst, me),
                send_sem=ss.at[p],
                recv_sem=rs.at[me],
                device_id=peer(p),
                device_id_type=MESH,
            )

        def here(o):
            q = lax.rem(me + group - o, group)
            return pltpu.make_async_remote_copy(
                src_ref=row(src, q),
                dst_ref=row(dst, q),
                send_sem=ss.at[q],
                recv_sem=rs.at[q],
                device_id=peer(q),
                device_id_type=MESH,
            )

        mine = pltpu.make_async_copy(row(src, me), row(dst, me), sem)

        def start():
            mine.start()
            lax.fori_loop(1, group, lambda o, c: (there(o).start(), c)[1], 0)

        def arrive():
            mine.wait()
            lax.fori_loop(1, group, lambda o, c: (here(o).wait_recv(), c)[1], 0)

        def leave():
            lax.fori_loop(1, group, lambda o, c: (there(o).wait_send(), c)[1], 0)

        return start, arrive, leave

    idx_start, idx_arrive, idx_leave = exchange(oidx, sidx, idx_ss, idx_rs, self_sem.at[0])
    st_start, st_arrive, st_leave = exchange(own, st, st_ss, st_rs, self_sem.at[1])
    b0_start, b0_arrive, b0_leave = exchange(
        back.at[pl.ds(0, 4)], ret.at[pl.ds(0, 4)], b0_ss, b0_rs, self_sem.at[2]
    )
    b1_start, b1_arrive, b1_leave = exchange(
        back.at[pl.ds(4, 4)], ret.at[pl.ds(4, 4)], b1_ss, b1_rs, self_sem.at[3]
    )

    sub = lax.broadcasted_iota(jnp.int32, (ROWS, LANES), 0)
    lane = lax.broadcasted_iota(jnp.int32, (ROWS, LANES), 1)
    eye = sub == lane

    def to_row(column):
        return jnp.sum(jnp.where(eye, column, 0.0), axis=0, keepdims=True)

    def to_column(line):
        return jnp.sum(jnp.where(eye, line, 0.0), axis=1, keepdims=True)

    def remote(src, dst, ss, rs, device):
        return pltpu.make_async_remote_copy(
            src_ref=src,
            dst_ref=dst,
            send_sem=ss,
            recv_sem=rs,
            device_id=device,
            device_id_type=MESH,
        )

    e_faces = [
        remote(ef.at[pl.ds(1, 2), pl.ds(0, CY), :], ex_r, eh_ss.at[0], eh_rs.at[0], down[0]),
        remote(ey_s, ey_r, eh_ss.at[1], eh_rs.at[1], down[1]),
        remote(ez_s, ez_r, eh_ss.at[2], eh_rs.at[2], down[2]),
    ]
    h_faces = [
        remote(
            hf.at[pl.ds(1, 2), pl.ds(ROWS - CY, CY), :], hx_r, hh_ss.at[0], hh_rs.at[0], up[0]
        ),
        remote(hy_s, hy_r, hh_ss.at[1], hh_rs.at[1], up[1]),
        remote(hz_s, hz_r, hh_ss.at[2], hh_rs.at[2], up[2]),
    ]
    live = [n > 1 for n in sizes]

    def pack_e():
        ey_s[0] = ef[0, pl.ds(0, CX, stride=CY), :]
        ey_s[1] = ef[2, pl.ds(0, CX, stride=CY), :]
        for i in range(2):
            ez_s[pl.ds(i, 1), :] = to_row(ef[i, :, 0:1])

    def pack_h():
        hy_s[0] = hf[0, pl.ds(CY - 1, CX, stride=CY), :]
        hy_s[1] = hf[2, pl.ds(CY - 1, CX, stride=CY), :]
        for i in range(2):
            hz_s[pl.ds(i, 1), :] = to_row(hf[i, :, LANES - 1 : LANES])

    def start_faces(faces):
        for face, on in zip(faces, live):
            if on:
                face.start()

    def arrive_faces(faces):
        for face, on in zip(faces, live):
            if on:
                face.wait_recv()

    def leave_faces(faces):
        for face, on in zip(faces, live):
            if on:
                face.wait_send()

    def edge(cond):
        return jnp.where(cond, 1.0, 0.0).astype(F32)

    e_edge = [edge(ax < n_gx - 1), edge(ay < n_gy - 1), edge(az < n_gz - 1)]
    h_edge = [edge(ax > 0), edge(ay > 0), edge(az > 0)]

    def spread(face):
        return jnp.broadcast_to(face[:, None, :], (CX, CY, LANES)).reshape(ROWS, LANES)

    def update_h(first):
        e = [ef[c] for c in range(3)]
        hx = [ex_r[i] * e_edge[0] if live[0] else jnp.zeros((CY, LANES), F32) for i in range(2)]
        hy = [ey_r[i] * e_edge[1] if live[1] else jnp.zeros((CX, LANES), F32) for i in range(2)]
        hz = [
            to_column(ez_r[pl.ds(i, 1), :]) * e_edge[2] if live[2] else jnp.zeros((ROWS, 1), F32)
            for i in range(2)
        ]
        x1 = jnp.concatenate([e[1][CY:], hx[0]], axis=0)
        x2 = jnp.concatenate([e[2][CY:], hx[1]], axis=0)
        last_y = lax.rem(sub, CY) == CY - 1
        y0 = jnp.where(last_y, spread(hy[0]), pltpu.roll(e[0], ROWS - 1, 0))
        y2 = jnp.where(last_y, spread(hy[1]), pltpu.roll(e[2], ROWS - 1, 0))
        last_z = lane == LANES - 1
        z0 = jnp.where(last_z, hz[0], pltpu.roll(e[0], LANES - 1, 1))
        z1 = jnp.where(last_z, hz[1], pltpu.roll(e[1], LANES - 1, 1))
        curl = (
            (y2 - e[2]) - (z1 - e[1]),
            (z0 - e[0]) - (x2 - e[2]),
            (x1 - e[1]) - (y0 - e[0]),
        )
        for c in range(3):
            if first:
                hf[c] = -DT * curl[c]
            else:
                hf[c] = hf[c] - DT * curl[c]

    def update_e(source):
        h = [hf[c] for c in range(3)]
        hx = [hx_r[i] * h_edge[0] if live[0] else jnp.zeros((CY, LANES), F32) for i in range(2)]
        hy = [hy_r[i] * h_edge[1] if live[1] else jnp.zeros((CX, LANES), F32) for i in range(2)]
        hz = [
            to_column(hz_r[pl.ds(i, 1), :]) * h_edge[2] if live[2] else jnp.zeros((ROWS, 1), F32)
            for i in range(2)
        ]
        x1 = jnp.concatenate([hx[0], h[1][: ROWS - CY]], axis=0)
        x2 = jnp.concatenate([hx[1], h[2][: ROWS - CY]], axis=0)
        first_y = lax.rem(sub, CY) == 0
        y0 = jnp.where(first_y, spread(hy[0]), pltpu.roll(h[0], 1, 0))
        y2 = jnp.where(first_y, spread(hy[1]), pltpu.roll(h[2], 1, 0))
        first_z = lane == 0
        z0 = jnp.where(first_z, hz[0], pltpu.roll(h[0], 1, 1))
        z1 = jnp.where(first_z, hz[1], pltpu.roll(h[1], 1, 1))
        curl = (
            (h[2] - y2) - (h[1] - z1),
            (h[0] - z0) - (h[2] - x2),
            (h[1] - x1) - (h[0] - y0),
        )
        for c in range(3):
            ef[c] = ef[c] + inv[...] * (DT * curl[c] - source[c])

    def build():
        cell = sidx[...]
        key = ((cell >> 13) << 7) | (cell & (LANES - 1))
        quo = (cell >> 7) & (HALF - 1)
        qsel[...] = quo
        key_t = jnp.transpose(
            jnp.concatenate([key, jnp.zeros((LANES - group, LANES), jnp.int32)], axis=0)
            if group < LANES
            else key
        )
        down_256 = lax.broadcasted_iota(jnp.int32, (2 * LANES, LANES), 0)
        across_256 = lax.broadcasted_iota(jnp.int32, (LANES, 2 * LANES), 1)
        down_64 = lax.broadcasted_iota(jnp.int32, (HALF, LANES), 0)
        for b in range(group):
            where = pl.ds(b * LANES, LANES)
            wide[:, where] = jnp.where(down_256 == key[b : b + 1, :], 1.0, 0.0).astype(BF16)
            tall[where, :] = jnp.where(across_256 == key_t[:, b : b + 1], 1.0, 0.0).astype(BF16)
            pick[:, where] = jnp.where(down_64 == quo[b : b + 1, :], 1.0, 0.0).astype(BF16)

    def coefficients():
        resonance, dephasing = st[8], st[9]
        damping = 0.5 * DT * dephasing
        stiffness = (resonance * DT) * (resonance * DT)
        recip = 1.0 / (1.0 + damping)
        coef[0] = (2.0 - stiffness) * recip
        coef[1] = (1.0 - damping) * recip
        coef[2] = st[10] * (DT * DT) * recip
        coef[3] = (DT * WORK_SHARE) / resonance

    def gather():
        for c in range(3):
            hi, lo = split(ef[c])
            for piece, part in enumerate((hi, lo)):
                rows = pl.ds((piece * 3 + c) * HALF, HALF)
                el[rows, 0:LANES] = part[:HALF]
                el[rows, LANES : 2 * LANES] = part[HALF:]
        down_64 = lax.broadcasted_iota(jnp.int32, (HALF, LANES), 0)
        for t in range(group // 2):
            found = jnp.dot(
                el[...], wide[:, pl.ds(t * 2 * LANES, 2 * LANES)], preferred_element_type=F32
            )
            for half in range(2):
                b = 2 * t + half
                chosen = down_64 == qsel[pl.ds(b, 1), :]
                for c in range(3):
                    both = (
                        found[c * HALF : (c + 1) * HALF, half * LANES : (half + 1) * LANES]
                        + found[
                            (3 + c) * HALF : (4 + c) * HALF, half * LANES : (half + 1) * LANES
                        ]
                    )
                    samp[c, pl.ds(b, 1), :] = jnp.sum(
                        jnp.where(chosen, both, 0.0), axis=0, keepdims=True
                    )

    def bloch(last):
        upper, pumped = st[6], st[7]
        lower = 1.0 - upper - pumped
        gain = coef[2] * (lower - upper)
        work = jnp.zeros((group, LANES), F32)
        changes = []
        for c in range(3):
            current, previous, sample = st[c], st[3 + c], samp[c]
            advanced = coef[0] * current - coef[1] * previous + gain * sample
            work = work + sample * (advanced - previous)
            changes.append(advanced - current)
            st[3 + c] = current
            st[c] = advanced
            if last:
                back[c] = current
                back[4 + c] = advanced
        pumped_new = pumped + DT * (st[11] * lower - PUMP_DECAY * pumped)
        upper_new = (
            upper + DT * (PUMP_DECAY * pumped - UPPER_DECAY * upper) + coef[3] * work
        )
        st[6] = upper_new
        st[7] = pumped_new
        if last:
            back[3] = pumped_new
            back[7] = upper_new
        return changes

    def scatter(changes):
        for c in range(3):
            for piece, part in enumerate(split(changes[c])):
                part = part.astype(F32)
                for b in range(group):
                    line = jnp.broadcast_to(part[b : b + 1, :], (CY, LANES)).astype(BF16)
                    amat[pl.ds((piece * 3 + c) * HALF, HALF), pl.ds(b * LANES, LANES)] = pick[
                        :, pl.ds(b * LANES, LANES)
                    ] * jnp.concatenate([line] * (HALF // CY), axis=0)
        total = jnp.dot(amat[...], tall[...], preferred_element_type=F32)
        total = total[: 3 * HALF] + total[3 * HALF :]
        return [
            jnp.concatenate(
                [
                    total[c * HALF : (c + 1) * HALF, :LANES],
                    total[c * HALF : (c + 1) * HALF, LANES:],
                ],
                axis=0,
            )
            for c in range(3)
        ]

    ez_s[...] = jnp.zeros_like(ez_s)
    hz_s[...] = jnp.zeros_like(hz_s)
    pack_e()
    kind = cls[...]
    inverse = jnp.zeros((ROWS, LANES), F32)
    for number, epsilon in enumerate(EPSILON):
        inverse = jnp.where(kind == number, 1.0 / epsilon, inverse)
    inv[...] = inverse

    pl.semaphore_wait(barrier, greetings)
    idx_start()
    start_faces(e_faces)
    st_start()

    for step in range(STEPS):
        if step == 0:
            arrive_faces(e_faces)
            update_h(True)
            pack_h()
            start_faces(h_faces)
            idx_arrive()
            build()
            gather()
            st_arrive()
            coefficients()
        else:
            gather()
            arrive_faces(e_faces)
            leave_faces(h_faces)
            update_h(False)
            pack_h()
            start_faces(h_faces)
        changes = bloch(step == STEPS - 1)
        if step == STEPS - 1:
            b0_start()
            b1_start()
        source = scatter(changes)
        arrive_faces(h_faces)
        leave_faces(e_faces)
        update_e(source)
        if step < STEPS - 1:
            pack_e()
            start_faces(e_faces)
    leave_faces(h_faces)

    outs = [
        pltpu.make_async_copy(ef, e_out, out_sem.at[0]),
        pltpu.make_async_copy(hf, h_out, out_sem.at[1]),
    ]
    for copy in outs:
        copy.start()
    b0_arrive()
    b1_arrive()
    more = [
        pltpu.make_async_copy(ret.at[pl.ds(4, 3)], pol_out.at[pl.ds(0, 3)], out_sem.at[2]),
        pltpu.make_async_copy(ret.at[pl.ds(0, 3)], pol_out.at[pl.ds(3, 3)], out_sem.at[3]),
        pltpu.make_async_copy(ret.at[7], pop_out.at[0], out_sem.at[4]),
        pltpu.make_async_copy(ret.at[3], pop_out.at[1], out_sem.at[5]),
    ]
    for copy in more:
        copy.start()
    idx_leave()
    st_leave()
    b0_leave()
    b1_leave()
    for copy in outs + more:
        copy.wait()


def shards(sizes, electric, classes, cells, polar, popul, res, dep, cou, pum):
    group = sizes[1] * sizes[2]
    cell_rows = (ROWS, LANES)
    plane = (group, LANES)
    dma = pltpu.SemaphoreType.DMA
    vmem = pltpu.VMEM
    any_spec = pl.BlockSpec(memory_space=pl.ANY)
    outs = pl.pallas_call(
        functools.partial(kernel, sizes),
        out_shape=(
            jax.ShapeDtypeStruct((3, *cell_rows), F32),
            jax.ShapeDtypeStruct((3, *cell_rows), F32),
            jax.ShapeDtypeStruct((6, *plane), F32),
            jax.ShapeDtypeStruct((2, *plane), F32),
        ),
        in_specs=[any_spec] * 9,
        out_specs=(any_spec,) * 4,
        scratch_shapes=[
            vmem((3, *cell_rows), F32),
            vmem((3, *cell_rows), F32),
            vmem(cell_rows, F32),
            vmem(cell_rows, jnp.int32),
            vmem((12, *plane), F32),
            vmem(plane, jnp.int32),
            vmem((12, *plane), F32),
            vmem(plane, jnp.int32),
            vmem((8, *plane), F32),
            vmem((8, *plane), F32),
            vmem((4, *plane), F32),
            vmem(plane, jnp.int32),
            vmem((2 * LANES, group * LANES), BF16),
            vmem((group * LANES, 2 * LANES), BF16),
            vmem((HALF, group * LANES), BF16),
            vmem((6 * HALF, 2 * LANES), BF16),
            vmem((6 * HALF, group * LANES), BF16),
            vmem((3, *plane), F32),
            vmem((2, CX, LANES), F32),
            vmem((8, LANES), F32),
            vmem((2, CX, LANES), F32),
            vmem((8, LANES), F32),
            vmem((2, CY, LANES), F32),
            vmem((2, CX, LANES), F32),
            vmem((8, LANES), F32),
            vmem((2, CY, LANES), F32),
            vmem((2, CX, LANES), F32),
            vmem((8, LANES), F32),
            dma((9,)),
            dma((4,)),
            dma((group,)),
            dma((group,)),
            dma((group,)),
            dma((group,)),
            dma((group,)),
            dma((group,)),
            dma((group,)),
            dma((group,)),
            dma((3,)),
            dma((3,)),
            dma((3,)),
            dma((3,)),
            dma((6,)),
        ],
        compiler_params=pltpu.CompilerParams(collective_id=0, has_side_effects=True),
        name="laser",
    )(
        electric.reshape(3, *cell_rows),
        classes.reshape(cell_rows),
        cells.reshape(plane),
        polar.reshape(6, *plane),
        popul.reshape(2, *plane),
        res.reshape(plane),
        dep.reshape(plane),
        cou.reshape(plane),
        pum.reshape(plane),
    )
    return (
        outs[0].reshape(electric.shape),
        outs[1].reshape(electric.shape),
        outs[2].reshape(polar.shape),
        outs[3].reshape(popul.shape),
    )


def solution(mesh):
    sizes = tuple(mesh.shape[axis] for axis in ("gx", "gy", "gz"))
    field = P(None, "gx", "gy", "gz")
    slots = P("gx", ("gy", "gz"), None)
    polar = P(None, None, "gx", ("gy", "gz"), None)
    popul = P(None, "gx", ("gy", "gz"), None)
    return jax.shard_map(
        functools.partial(shards, sizes),
        mesh=mesh,
        in_specs=(
            field,
            P("gx", "gy", "gz"),
            slots,
            polar,
            popul,
            slots,
            slots,
            slots,
            slots,
        ),
        out_specs=(field, field, polar, popul),
        check_vma=False,
    )
```

time: 434 us -> 54 us (0.12); the launches traced: 428 us -> 53.8 us
  other arithmetic: 126 us -> 0 us
  starting transfers between devices: 125 us -> 0 us
  local copies, waits for them, and re-layouts: 121 us -> 3.99 us
  waiting for transfers between devices: 53.8 us -> 0 us
  Pallas kernels: 0 us -> 49.1 us
    scatter-add x4 -> x0, other arithmetic: 106 us -> none  [shards(): jnp.zeros((3, cell_count), jnp.float32).at[:, dropped]]
    ppermute x24 -> x0, starting transfers between devices: 69 us -> none  [the longest x12 50.1 us: extended_2(): lax.ppermute(lax.slice_in_dim(block, block.shape[dim] - width, None, axis...]
    gather x8 -> x0, local copies, waits for them, and re-layouts: 68.9 us -> none  [shards(): electric.reshape(3, -1)[:, safe_index] * weight]
    all_to_all x9 -> x0, starting transfers between devices: 56.1 us -> none  [the longest x4 27.8 us: shards(): lax.all_to_all(change, ('gy', 'gz'), split_axis=2, concat_axis=2, tiled=T...]
    pallas_call x0 -> x1, Pallas kernels: none -> 49.1 us  [shards(): pl.pallas_call(functools.partial(kernel, sizes), out_shape=(jax.ShapeDtyp...]
    all_to_all x9 -> x0, waiting for transfers between devices: 27.3 us -> none  [the longest x4 27.3 us: shards(): lax.all_to_all(change, ('gy', 'gz'), split_axis=2, concat_axis=2, tiled=T...]
    ppermute x24 -> x0, waiting for transfers between devices: 26.5 us -> none  [the longest x12 23.8 us: extended_2(): lax.ppermute(lax.slice_in_dim(block, 0, width, axis=dim), axis, backward)]
    reshape x8 -> x0, local copies, waits for them, and re-layouts: 26.2 us -> none  [the longest x4 21 us: shards(): summed.reshape(3, width_x, width_y, width_z)]
  transfers between devices with their start and end apart: 33 -> 0, of which waited for: 11 -> 0; matrix products, arithmetic and copies ran while one was open for 25% -> 0% of each run, Pallas kernels for 0% -> 0%
where the time goes in v1:
time: 54 us; the launch traced here: 53.8 us
  Pallas kernels  49.1 us (91%)
  local copies, waits for them, and re-layouts  3.99 us (7%)
  between operations  0.65 us (1%)
    pallas_call x1, Pallas kernels, shards(): pl.pallas_call(functools.partial(kernel, sizes), out_shape=(jax.ShapeDtyp...  49.1 us
    unnamed x10, local copies, waits for them, and re-layouts  3.99 us

profile of v1, /device:TPU:1, one launch (start us, length us, event | category | flops | bytes accessed | tf_op | source)
XLA Modules:
  0.0 53.8 jit_solution(847905157731568798)
XLA Ops:
  0.6 49.1 %laser.1 = (f32[3,128,128]{2,1,0:T(8,128)}, f32[3,128,128]{2,1,0:T(8,128)}, f32[6,32,128]{2,1,0:T(8,128)}, f32[2,32,128]{2,1,0:T(8,128)}) custom-call(f32[3,128,128]{2,1,0:T(8,128)} %bitcast.19, s32[128,128]{1,0:T(8,128)} %bitcast.22, s32[32,128]{1,0:T(8,128)} %bitcast.25, f32[6,32,128]{2,1,0:T(8,128)} %bitcast.21, f32[2,32,128]{2,1,0:T(8,128)} %bitcast.24, ...), custom_call_target="tpu_custom_call" | custom-call | tf_op jit(solution)/shard_map/laser/pallas_call | solution.py:499
  49.8 0.0 copy-start
  49.8 1.7 %copy.19 = f32[3,8,16,128]{3,2,1,0:T(8,128)} copy(f32[3,8,16,128]{3,2,1,0:T(8,128)} %bitcast.18) | data formatting | bytes 393216
  51.5 0.0 copy-done
  51.5 0.0 copy-start.1
  51.5 0.7 %copy.20 = f32[3,8,16,128]{3,2,1,0:T(8,128)} copy(f32[3,8,16,128]{3,2,1,0:T(8,128)S(1)} %bitcast.17) | data formatting | bytes 393216
  52.1 0.3 copy-done.1
  52.4 0.0 copy-start.2
  52.4 0.6 %copy.21 = f32[2,3,1,32,128]{4,3,2,1,0:T(8,128)} copy(f32[2,3,1,32,128]{4,3,2,1,0:T(8,128)S(1)} %bitcast.20) | data formatting | bytes 196608
  53.1 0.1 copy-done.2
  53.2 0.6 %copy.22 = f32[2,1,32,128]{3,2,1,0:T(8,128)} copy(f32[2,1,32,128]{3,2,1,0:T(8,128)S(1)} %bitcast.23) | data formatting | bytes 65536
Async XLA Ops:
  49.8 1.7 %copy-start = (f32[3,128,128]{2,1,0:T(8,128)S(1)}, f32[3,128,128]{2,1,0:T(8,128)}, u32[]{:S(2)}) copy-start(f32[3,128,128]{2,1,0:T(8,128)} %get-tuple-element.9) | copy-start | bytes 589828
  51.5 1.0 %copy-start.1 = (f32[6,32,128]{2,1,0:T(8,128)S(1)}, f32[6,32,128]{2,1,0:T(8,128)}, u32[]{:S(2)}) copy-start(f32[6,32,128]{2,1,0:T(8,128)} %get-tuple-element.10) | copy-start | bytes 294916
  52.4 0.8 %copy-start.2 = (f32[2,32,128]{2,1,0:T(8,128)S(1)}, f32[2,32,128]{2,1,0:T(8,128)}, u32[]{:S(2)}) copy-start(f32[2,32,128]{2,1,0:T(8,128)} %get-tuple-element.11) | copy-start | bytes 98308

commit v2 on v1

--- a/solution.py
+++ b/solution.py
@@ -59,7 +59,6 @@
     tall,
     pick,
     el,
-    amat,
     samp,
     ey_s,
     ez_s,
@@ -345,7 +344,7 @@
         coef[2] = st[10] * (DT * DT) * recip
         coef[3] = (DT * WORK_SHARE) / resonance
 
-    def gather():
+    def gather(accs):
         for c in range(3):
             hi, lo = split(ef[c])
             for piece, part in enumerate((hi, lo)):
@@ -353,23 +352,27 @@
                 el[rows, 0:LANES] = part[:HALF]
                 el[rows, LANES : 2 * LANES] = part[HALF:]
         down_64 = lax.broadcasted_iota(jnp.int32, (HALF, LANES), 0)
-        for t in range(group // 2):
-            found = jnp.dot(
-                el[...], wide[:, pl.ds(t * 2 * LANES, 2 * LANES)], preferred_element_type=F32
-            )
+
+        def collect(t):
+            found = pltpu.matmul_pop(accs[t % 4])
             for half in range(2):
                 b = 2 * t + half
                 chosen = down_64 == qsel[pl.ds(b, 1), :]
                 for c in range(3):
-                    both = (
-                        found[c * HALF : (c + 1) * HALF, half * LANES : (half + 1) * LANES]
-                        + found[
-                            (3 + c) * HALF : (4 + c) * HALF, half * LANES : (half + 1) * LANES
-                        ]
-                    )
+                    both = found[c * HALF : (c + 1) * HALF, half * LANES : (half + 1) * LANES]
                     samp[c, pl.ds(b, 1), :] = jnp.sum(
                         jnp.where(chosen, both, 0.0), axis=0, keepdims=True
                     )
+
+        for t in range(group // 2):
+            mxu, reg, acc = t % 2, (t // 2) % 2, accs[t % 4]
+            pltpu.matmul_push_rhs(wide[:, pl.ds(t * 2 * LANES, 2 * LANES)], reg, mxu)
+            pltpu.matmul_acc_lhs(acc, el[: 3 * HALF], load_staged_rhs=reg)
+            pltpu.matmul_acc_lhs(acc, el[3 * HALF :])
+            if t >= 2:
+                collect(t - 2)
+        for t in range(group // 2 - 2, group // 2):
+            collect(t)
 
     def bloch(last):
         upper, pumped = st[6], st[7]
@@ -398,17 +401,32 @@
             back[7] = upper_new
         return changes
 
-    def scatter(changes):
-        for c in range(3):
-            for piece, part in enumerate(split(changes[c])):
-                part = part.astype(F32)
-                for b in range(group):
-                    line = jnp.broadcast_to(part[b : b + 1, :], (CY, LANES)).astype(BF16)
-                    amat[pl.ds((piece * 3 + c) * HALF, HALF), pl.ds(b * LANES, LANES)] = pick[
-                        :, pl.ds(b * LANES, LANES)
-                    ] * jnp.concatenate([line] * (HALF // CY), axis=0)
-        total = jnp.dot(amat[...], tall[...], preferred_element_type=F32)
-        total = total[: 3 * HALF] + total[3 * HALF :]
+    def scatter(changes, accs):
+        parts = [split(change) for change in changes]
+        parts = [[part[piece].astype(F32) for part in parts] for piece in range(2)]
+        for t in range(group // 2):
+            mxu, reg, acc = t % 2, (t // 2) % 2, accs[t % 2]
+            pltpu.matmul_push_rhs(tall[pl.ds(t * 2 * LANES, 2 * LANES), :], reg, mxu)
+            for piece in range(2):
+                rows = []
+                for c in range(3):
+                    cols = []
+                    for half in range(2):
+                        b = 2 * t + half
+                        line = jnp.broadcast_to(
+                            parts[piece][c][b : b + 1, :], (CY, LANES)
+                        ).astype(BF16)
+                        cols.append(
+                            pick[:, pl.ds(b * LANES, LANES)]
+                            * jnp.concatenate([line] * (HALF // CY), axis=0)
+                        )
+                    rows.append(jnp.concatenate(cols, axis=1))
+                lhs = jnp.concatenate(rows, axis=0)
+                if piece == 0:
+                    pltpu.matmul_acc_lhs(acc, lhs, load_staged_rhs=reg)
+                else:
+                    pltpu.matmul_acc_lhs(acc, lhs)
+        total = pltpu.matmul_pop(accs[0]) + pltpu.matmul_pop(accs[1])
         return [
             jnp.concatenate(
                 [
@@ -434,35 +452,40 @@
     start_faces(e_faces)
     st_start()
 
-    for step in range(STEPS):
-        if step == 0:
-            arrive_faces(e_faces)
-            update_h(True)
-            pack_h()
-            start_faces(h_faces)
-            idx_arrive()
-            build()
-            gather()
-            st_arrive()
-            coefficients()
-        else:
-            gather()
-            arrive_faces(e_faces)
-            leave_faces(h_faces)
-            update_h(False)
-            pack_h()
-            start_faces(h_faces)
-        changes = bloch(step == STEPS - 1)
-        if step == STEPS - 1:
-            b0_start()
-            b1_start()
-        source = scatter(changes)
-        arrive_faces(h_faces)
-        leave_faces(e_faces)
-        update_e(source)
-        if step < STEPS - 1:
-            pack_e()
-            start_faces(e_faces)
+    def steps(*accs):
+        for step in range(STEPS):
+            if step == 0:
+                arrive_faces(e_faces)
+                update_h(True)
+                pack_h()
+                start_faces(h_faces)
+                idx_arrive()
+                build()
+                gather(accs)
+                st_arrive()
+                coefficients()
+            else:
+                gather(accs)
+                arrive_faces(e_faces)
+                leave_faces(h_faces)
+                update_h(False)
+                pack_h()
+                start_faces(h_faces)
+            changes = bloch(step == STEPS - 1)
+            if step == STEPS - 1:
+                b0_start()
+                b1_start()
+            source = scatter(changes, accs)
+            arrive_faces(h_faces)
+            leave_faces(e_faces)
+            update_e(source)
+            if step < STEPS - 1:
+                pack_e()
+                start_faces(e_faces)
+
+    pl.run_scoped(
+        steps, *[pltpu.ACC(i % 2)((3 * HALF, 2 * LANES), F32) for i in range(4)]
+    )
     leave_faces(h_faces)
 
     outs = [
@@ -523,7 +546,6 @@
             vmem((group * LANES, 2 * LANES), BF16),
             vmem((HALF, group * LANES), BF16),
             vmem((6 * HALF, 2 * LANES), BF16),
-            vmem((6 * HALF, group * LANES), BF16),
             vmem((3, *plane), F32),
             vmem((2, CX, LANES), F32),
             vmem((8, LANES), F32),

time: 54 us -> 53.3 us (0.987)
  Pallas kernels: 49.1 us -> 48.4 us
    pallas_call x1, Pallas kernels: 49.1 us -> 48.4 us  [shards(): pl.pallas_call(functools.partial(kernel, sizes), out_shape=(jax.ShapeDtyp...]
where the time goes in v2:
time: 53.3 us; the launch traced here: 53.1 us
  Pallas kernels  48.4 us (91%)
  local copies, waits for them, and re-layouts  3.99 us (7%)
  between operations  0.65 us (1%)
    pallas_call x1, Pallas kernels, shards(): pl.pallas_call(functools.partial(kernel, sizes), out_shape=(jax.ShapeDtyp...  48.4 us
    unnamed x10, local copies, waits for them, and re-layouts  3.99 us

profile of v2, /device:TPU:1, one launch (start us, length us, event | category | flops | bytes accessed | tf_op | source)
XLA Modules:
  0.0 53.1 jit_solution(4071912275834646700)
XLA Ops:
  0.6 48.4 %laser.1 = (f32[3,128,128]{2,1,0:T(8,128)}, f32[3,128,128]{2,1,0:T(8,128)}, f32[6,32,128]{2,1,0:T(8,128)}, f32[2,32,128]{2,1,0:T(8,128)}) custom-call(f32[3,128,128]{2,1,0:T(8,128)} %bitcast.19, s32[128,128]{1,0:T(8,128)} %bitcast.22, s32[32,128]{1,0:T(8,128)} %bitcast.25, f32[6,32,128]{2,1,0:T(8,128)} %bitcast.21, f32[2,32,128]{2,1,0:T(8,128)} %bitcast.24, ...), custom_call_target="tpu_custom_call" | custom-call | tf_op jit(solution)/shard_map/laser/pallas_call | solution.py:522
  49.0 0.0 copy-start
  49.1 1.7 %copy.19 = f32[3,8,16,128]{3,2,1,0:T(8,128)} copy(f32[3,8,16,128]{3,2,1,0:T(8,128)} %bitcast.18) | data formatting | bytes 393216
  50.7 0.0 copy-done
  50.7 0.0 copy-start.1
  50.7 0.7 %copy.20 = f32[3,8,16,128]{3,2,1,0:T(8,128)} copy(f32[3,8,16,128]{3,2,1,0:T(8,128)S(1)} %bitcast.17) | data formatting | bytes 393216
  51.4 0.3 copy-done.1
  51.7 0.0 copy-start.2
  51.7 0.6 %copy.21 = f32[2,3,1,32,128]{4,3,2,1,0:T(8,128)} copy(f32[2,3,1,32,128]{4,3,2,1,0:T(8,128)S(1)} %bitcast.20) | data formatting | bytes 196608
  52.3 0.1 copy-done.2
  52.4 0.6 %copy.22 = f32[2,1,32,128]{3,2,1,0:T(8,128)} copy(f32[2,1,32,128]{3,2,1,0:T(8,128)S(1)} %bitcast.23) | data formatting | bytes 65536
Async XLA Ops:
  49.0 1.7 %copy-start = (f32[3,128,128]{2,1,0:T(8,128)S(1)}, f32[3,128,128]{2,1,0:T(8,128)}, u32[]{:S(2)}) copy-start(f32[3,128,128]{2,1,0:T(8,128)} %get-tuple-element.9) | copy-start | bytes 589828
  50.7 1.0 %copy-start.1 = (f32[6,32,128]{2,1,0:T(8,128)S(1)}, f32[6,32,128]{2,1,0:T(8,128)}, u32[]{:S(2)}) copy-start(f32[6,32,128]{2,1,0:T(8,128)} %get-tuple-element.10) | copy-start | bytes 294916
  51.7 0.8 %copy-start.2 = (f32[2,32,128]{2,1,0:T(8,128)S(1)}, f32[2,32,128]{2,1,0:T(8,128)}, u32[]{:S(2)}) copy-start(f32[2,32,128]{2,1,0:T(8,128)} %get-tuple-element.11) | copy-start | bytes 98308

commit v3 on v2

--- a/solution.py
+++ b/solution.py
@@ -28,6 +28,10 @@
     return hi, (x - hi.astype(F32)).astype(BF16)
 
 
+def wrap(i, n):
+    return jnp.where(i >= n, i - n, i)
+
+
 def kernel(
     sizes,
     e_in,
@@ -39,12 +43,9 @@
     dep_in,
     cou_in,
     pum_in,
-    e_out,
-    h_out,
-    pol_out,
-    pop_out,
     ef,
     hf,
+    ret,
     inv,
     cls,
     own,
@@ -52,7 +53,6 @@
     st,
     sidx,
     back,
-    ret,
     coef,
     qsel,
     wide,
@@ -84,7 +84,6 @@
     eh_rs,
     hh_ss,
     hh_rs,
-    out_sem,
 ):
     n_gx, n_gy, n_gz = sizes
     group = n_gy * n_gz
@@ -103,8 +102,15 @@
         (ax, ay, lax.rem(az + 1, n_gz)),
     )
 
-    def peer(p):
-        return (ax, p // n_gz, lax.rem(p, n_gz))
+    ys = [wrap(ay + d, n_gy) for d in range(n_gy)]
+    zs = [wrap(az + d, n_gz) for d in range(n_gz)]
+
+    def far(offset):
+        dy, dz = offset
+        return -2 * min(dy, n_gy - dy) - min(dz, n_gz - dz)
+
+    offsets = [(dy, dz) for dy in range(n_gy) for dz in range(n_gz) if dy or dz]
+    peers = [(ys[dy], zs[dz]) for dy, dz in sorted(offsets, key=far)]
 
     loads = (
         (idx_in, oidx),
@@ -126,13 +132,8 @@
 
     barrier = pltpu.get_barrier_semaphore()
 
-    def greet(o, carry):
-        pl.semaphore_signal(
-            barrier, inc=1, device_id=peer(lax.rem(me + o, group)), device_id_type=MESH
-        )
-        return carry
-
-    lax.fori_loop(1, group, greet, 0)
+    for y, z in peers:
+        pl.semaphore_signal(barrier, inc=1, device_id=(ax, y, z), device_id_type=MESH)
     greetings = group - 1
     if n_gx > 1:
         for other in (down[0], up[0]):
@@ -148,40 +149,36 @@
         return buf.at[:, pl.ds(p, 1), :]
 
     def exchange(src, dst, ss, rs, sem):
-        def there(o):
-            p = lax.rem(me + o, group)
-            return pltpu.make_async_remote_copy(
-                src_ref=row(src, p),
-                dst_ref=row(dst, me),
-                send_sem=ss.at[p],
-                recv_sem=rs.at[me],
-                device_id=peer(p),
-                device_id_type=MESH,
-            )
-
-        def here(o):
-            q = lax.rem(me + group - o, group)
-            return pltpu.make_async_remote_copy(
-                src_ref=row(src, q),
-                dst_ref=row(dst, q),
-                send_sem=ss.at[q],
-                recv_sem=rs.at[q],
-                device_id=peer(q),
-                device_id_type=MESH,
-            )
-
         mine = pltpu.make_async_copy(row(src, me), row(dst, me), sem)
+        out, back = [], []
+        for y, z in peers:
+            p = y * n_gz + z
+            ends = ((row(src, p), row(dst, me), rs.at[me]), (row(src, p), row(dst, p), rs.at[p]))
+            for copies, (from_ref, to_ref, recv) in zip((out, back), ends):
+                copies.append(
+                    pltpu.make_async_remote_copy(
+                        src_ref=from_ref,
+                        dst_ref=to_ref,
+                        send_sem=ss.at[p],
+                        recv_sem=recv,
+                        device_id=(ax, y, z),
+                        device_id_type=MESH,
+                    )
+                )
 
         def start():
             mine.start()
-            lax.fori_loop(1, group, lambda o, c: (there(o).start(), c)[1], 0)
+            for copy in out:
+                copy.start()
 
         def arrive():
             mine.wait()
-            lax.fori_loop(1, group, lambda o, c: (here(o).wait_recv(), c)[1], 0)
+            for copy in back:
+                copy.wait_recv()
 
         def leave():
-            lax.fori_loop(1, group, lambda o, c: (there(o).wait_send(), c)[1], 0)
+            for copy in out:
+                copy.wait_send()
 
         return start, arrive, leave
 
@@ -374,6 +371,13 @@
         for t in range(group // 2 - 2, group // 2):
             collect(t)
 
+    def early():
+        upper, pumped = st[6], st[7]
+        lower = 1.0 - upper - pumped
+        for c in range(3):
+            back[c] = st[c]
+        back[3] = pumped + DT * (st[11] * lower - PUMP_DECAY * pumped)
+
     def bloch(last):
         upper, pumped = st[6], st[7]
         lower = 1.0 - upper - pumped
@@ -388,7 +392,6 @@
             st[3 + c] = current
             st[c] = advanced
             if last:
-                back[c] = current
                 back[4 + c] = advanced
         pumped_new = pumped + DT * (st[11] * lower - PUMP_DECAY * pumped)
         upper_new = (
@@ -397,7 +400,6 @@
         st[6] = upper_new
         st[7] = pumped_new
         if last:
-            back[3] = pumped_new
             back[7] = upper_new
         return changes
 
@@ -465,6 +467,9 @@
                 st_arrive()
                 coefficients()
             else:
+                if step == STEPS - 1:
+                    early()
+                    b0_start()
                 gather(accs)
                 arrive_faces(e_faces)
                 leave_faces(h_faces)
@@ -473,7 +478,6 @@
                 start_faces(h_faces)
             changes = bloch(step == STEPS - 1)
             if step == STEPS - 1:
-                b0_start()
                 b1_start()
             source = scatter(changes, accs)
             arrive_faces(h_faces)
@@ -488,27 +492,26 @@
     )
     leave_faces(h_faces)
 
-    outs = [
-        pltpu.make_async_copy(ef, e_out, out_sem.at[0]),
-        pltpu.make_async_copy(hf, h_out, out_sem.at[1]),
-    ]
-    for copy in outs:
-        copy.start()
     b0_arrive()
     b1_arrive()
-    more = [
-        pltpu.make_async_copy(ret.at[pl.ds(4, 3)], pol_out.at[pl.ds(0, 3)], out_sem.at[2]),
-        pltpu.make_async_copy(ret.at[pl.ds(0, 3)], pol_out.at[pl.ds(3, 3)], out_sem.at[3]),
-        pltpu.make_async_copy(ret.at[7], pop_out.at[0], out_sem.at[4]),
-        pltpu.make_async_copy(ret.at[3], pop_out.at[1], out_sem.at[5]),
-    ]
-    for copy in more:
-        copy.start()
     idx_leave()
     st_leave()
     b0_leave()
     b1_leave()
-    for copy in outs + more:
+
+
+def write(ef, hf, ret, e_out, h_out, pol_out, pop_out, sem):
+    copies = [
+        pltpu.make_async_copy(ef, e_out, sem.at[0]),
+        pltpu.make_async_copy(hf, h_out, sem.at[1]),
+        pltpu.make_async_copy(ret.at[pl.ds(4, 3)], pol_out.at[pl.ds(0, 3)], sem.at[2]),
+        pltpu.make_async_copy(ret.at[pl.ds(0, 3)], pol_out.at[pl.ds(3, 3)], sem.at[3]),
+        pltpu.make_async_copy(ret.at[7], pop_out.at[0], sem.at[4]),
+        pltpu.make_async_copy(ret.at[3], pop_out.at[1], sem.at[5]),
+    ]
+    for copy in copies:
+        copy.start()
+    for copy in copies:
         copy.wait()
 
 
@@ -519,26 +522,23 @@
     dma = pltpu.SemaphoreType.DMA
     vmem = pltpu.VMEM
     any_spec = pl.BlockSpec(memory_space=pl.ANY)
-    outs = pl.pallas_call(
+    vmem_spec = pl.BlockSpec(memory_space=pltpu.VMEM)
+    held = pl.pallas_call(
         functools.partial(kernel, sizes),
         out_shape=(
-            jax.ShapeDtypeStruct((3, *cell_rows), F32),
-            jax.ShapeDtypeStruct((3, *cell_rows), F32),
-            jax.ShapeDtypeStruct((6, *plane), F32),
-            jax.ShapeDtypeStruct((2, *plane), F32),
+            vmem((3, *cell_rows), F32),
+            vmem((3, *cell_rows), F32),
+            vmem((8, *plane), F32),
         ),
         in_specs=[any_spec] * 9,
-        out_specs=(any_spec,) * 4,
+        out_specs=(vmem_spec,) * 3,
         scratch_shapes=[
-            vmem((3, *cell_rows), F32),
-            vmem((3, *cell_rows), F32),
             vmem(cell_rows, F32),
             vmem(cell_rows, jnp.int32),
             vmem((12, *plane), F32),
             vmem(plane, jnp.int32),
             vmem((12, *plane), F32),
             vmem(plane, jnp.int32),
-            vmem((8, *plane), F32),
             vmem((8, *plane), F32),
             vmem((4, *plane), F32),
             vmem(plane, jnp.int32),
@@ -571,7 +571,6 @@
             dma((3,)),
             dma((3,)),
             dma((3,)),
-            dma((6,)),
         ],
         compiler_params=pltpu.CompilerParams(collective_id=0, has_side_effects=True),
         name="laser",
@@ -586,6 +585,19 @@
         cou.reshape(plane),
         pum.reshape(plane),
     )
+    outs = pl.pallas_call(
+        write,
+        out_shape=(
+            jax.ShapeDtypeStruct((3, *cell_rows), F32),
+            jax.ShapeDtypeStruct((3, *cell_rows), F32),
+            jax.ShapeDtypeStruct((6, *plane), F32),
+            jax.ShapeDtypeStruct((2, *plane), F32),
+        ),
+        in_specs=[vmem_spec] * 3,
+        out_specs=(any_spec,) * 4,
+        scratch_shapes=[dma((6,))],
+        name="write",
+    )(*[pltpu.with_memory_space_constraint(x, pltpu.VMEM) for x in held])
     return (
         outs[0].reshape(electric.shape),
         outs[1].reshape(electric.shape),

time: 53.3 us -> 47.3 us (0.89)
  local copies, waits for them, and re-layouts: 3.99 us -> 0 us
  Pallas kernels: 48.4 us -> 46.4 us
    unnamed x10 -> x0, local copies, waits for them, and re-layouts: 3.99 us -> none
    pallas_call x1 -> x2, Pallas kernels: 48.4 us -> 46.4 us  [the longest x1 45.6 us: shards(): pl.pallas_call(functools.partial(kernel, sizes), out_shape=(vmem((3, *cel...]
where the time goes in v3:
time: 47.3 us; the launch traced here: 47.1 us
  Pallas kernels  46.4 us (98%)
  between operations  0.64 us (1%)
    pallas_call x1, Pallas kernels, shards(): pl.pallas_call(functools.partial(kernel, sizes), out_shape=(vmem((3, *cel...  45.6 us

profile of v3, /device:TPU:1, one launch (start us, length us, event | category | flops | bytes accessed | tf_op | source)
XLA Modules:
  0.0 47.1 jit_solution(10575628192701155052)
XLA Ops:
  0.6 45.6 %laser.1 = (f32[3,128,128]{2,1,0:T(8,128)S(1)}, f32[3,128,128]{2,1,0:T(8,128)S(1)}, f32[8,32,128]{2,1,0:T(8,128)S(1)}) custom-call(f32[3,128,128]{2,1,0:T(8,128)} %bitcast.17, s32[128,128]{1,0:T(8,128)} %bitcast.19, s32[32,128]{1,0:T(8,128)} %bitcast.21, f32[6,32,128]{2,1,0:T(8,128)} %bitcast.18, f32[2,32,128]{2,1,0:T(8,128)} %bitcast.20, ...), custom_call_target="tpu_custom_call" | custom-call | tf_op jit(solution)/shard_map/laser/pallas_call | solution.py:526
  46.3 0.8 %write.1 = (f32[3,128,128]{2,1,0:T(8,128)}, f32[3,128,128]{2,1,0:T(8,128)}, f32[6,32,128]{2,1,0:T(8,128)}, f32[2,32,128]{2,1,0:T(8,128)}) custom-call(f32[3,128,128]{2,1,0:T(8,128)S(1)} %get-tuple-element.11.ef, f32[3,128,128]{2,1,0:T(8,128)S(1)} %get-tuple-element.12.hf, f32[8,32,128]{2,1,0:T(8,128)S(1)} %get-tuple-element.13.ret), custom_call_target="tpu_custom_call" | custom-call | tf_op jit(solution)/shard_map/write/pallas_call | solution.py:588

commit v4 on v3

--- a/solution.py
+++ b/solution.py
@@ -21,6 +21,15 @@
 HALF = 64
 CY = 16
 CX = 8
+
+
+NEAR = [
+    (dx, dy, dz)
+    for dx in (-1, 0, 1)
+    for dy in (-1, 0, 1)
+    for dz in (-1, 0, 1)
+    if (dx + dy + dz == 0 and (dx or dy)) or abs(dx) + abs(dy) + abs(dz) == 1
+]
 
 
 def split(x):
@@ -60,16 +69,25 @@
     pick,
     el,
     samp,
-    ey_s,
-    ez_s,
-    hy_s,
-    hz_s,
-    ex_r,
-    ey_r,
-    ez_r,
-    hx_r,
-    hy_r,
-    hz_r,
+    ydn,
+    yup,
+    zdn,
+    zup,
+    hx,
+    hy,
+    hz,
+    xp_r,
+    yp_r,
+    zp_r,
+    xm_r,
+    ym_r,
+    zm_r,
+    xz_r,
+    xy_r,
+    yz_r,
+    yx_r,
+    zy_r,
+    zx_r,
     load_sem,
     self_sem,
     idx_ss,
@@ -80,10 +98,8 @@
     b0_rs,
     b1_ss,
     b1_rs,
-    eh_ss,
-    eh_rs,
-    hh_ss,
-    hh_rs,
+    face_ss,
+    face_rs,
 ):
     n_gx, n_gy, n_gz = sizes
     group = n_gy * n_gz
@@ -91,16 +107,13 @@
     ay = lax.axis_index("gy")
     az = lax.axis_index("gz")
     me = ay * n_gz + az
-    down = (
-        (lax.rem(ax + n_gx - 1, n_gx), ay, az),
-        (ax, lax.rem(ay + n_gy - 1, n_gy), az),
-        (ax, ay, lax.rem(az + n_gz - 1, n_gz)),
-    )
-    up = (
-        (lax.rem(ax + 1, n_gx), ay, az),
-        (ax, lax.rem(ay + 1, n_gy), az),
-        (ax, ay, lax.rem(az + 1, n_gz)),
-    )
+
+    def near(dx, dy, dz):
+        return (
+            wrap(ax + dx % n_gx, n_gx),
+            wrap(ay + dy % n_gy, n_gy),
+            wrap(az + dz % n_gz, n_gz),
+        )
 
     ys = [wrap(ay + d, n_gy) for d in range(n_gy)]
     zs = [wrap(az + d, n_gz) for d in range(n_gz)]
@@ -135,10 +148,10 @@
     for y, z in peers:
         pl.semaphore_signal(barrier, inc=1, device_id=(ax, y, z), device_id_type=MESH)
     greetings = group - 1
-    if n_gx > 1:
-        for other in (down[0], up[0]):
-            pl.semaphore_signal(barrier, inc=1, device_id=other, device_id_type=MESH)
-        greetings += 2
+    across = [d for d in NEAR if d[0]]
+    for d in across:
+        pl.semaphore_signal(barrier, inc=1, device_id=near(*d), device_id_type=MESH)
+    greetings += len(across)
 
     for copy in loads:
         copy.wait()
@@ -201,109 +214,152 @@
     def to_column(line):
         return jnp.sum(jnp.where(eye, line, 0.0), axis=1, keepdims=True)
 
-    def remote(src, dst, ss, rs, device):
-        return pltpu.make_async_remote_copy(
-            src_ref=src,
-            dst_ref=dst,
-            send_sem=ss,
-            recv_sem=rs,
-            device_id=device,
-            device_id_type=MESH,
-        )
-
-    e_faces = [
-        remote(ef.at[pl.ds(1, 2), pl.ds(0, CY), :], ex_r, eh_ss.at[0], eh_rs.at[0], down[0]),
-        remote(ey_s, ey_r, eh_ss.at[1], eh_rs.at[1], down[1]),
-        remote(ez_s, ez_r, eh_ss.at[2], eh_rs.at[2], down[2]),
-    ]
-    h_faces = [
-        remote(
-            hf.at[pl.ds(1, 2), pl.ds(ROWS - CY, CY), :], hx_r, hh_ss.at[0], hh_rs.at[0], up[0]
-        ),
-        remote(hy_s, hy_r, hh_ss.at[1], hh_rs.at[1], up[1]),
-        remote(hz_s, hz_r, hh_ss.at[2], hh_rs.at[2], up[2]),
-    ]
-    live = [n > 1 for n in sizes]
-
-    def pack_e():
-        ey_s[0] = ef[0, pl.ds(0, CX, stride=CY), :]
-        ey_s[1] = ef[2, pl.ds(0, CX, stride=CY), :]
-        for i in range(2):
-            ez_s[pl.ds(i, 1), :] = to_row(ef[i, :, 0:1])
-
-    def pack_h():
-        hy_s[0] = hf[0, pl.ds(CY - 1, CX, stride=CY), :]
-        hy_s[1] = hf[2, pl.ds(CY - 1, CX, stride=CY), :]
-        for i in range(2):
-            hz_s[pl.ds(i, 1), :] = to_row(hf[i, :, LANES - 1 : LANES])
-
-    def start_faces(faces):
-        for face, on in zip(faces, live):
-            if on:
-                face.start()
-
-    def arrive_faces(faces):
-        for face, on in zip(faces, live):
-            if on:
-                face.wait_recv()
-
-    def leave_faces(faces):
-        for face, on in zip(faces, live):
-            if on:
-                face.wait_send()
+    def faces(step):
+        sends = (
+            (zdn, xz_r, (1, 0, -1)),
+            (ef.at[0, pl.ds(ROWS - CY, 8), :], xy_r, (1, -1, 0)),
+            (zdn, yz_r, (0, 1, -1)),
+            (ef.at[1, pl.ds(CY - 8, 8), :], yx_r, (-1, 1, 0)),
+            (zup, zy_r, (0, -1, 1)),
+            (zup, zx_r, (-1, 0, 1)),
+            (ef.at[pl.ds(1, 2), pl.ds(0, CY), :], xp_r, (-1, 0, 0)),
+            (ef.at[:, pl.ds(ROWS - CY, CY), :], xm_r, (1, 0, 0)),
+            (ydn, yp_r, (0, -1, 0)),
+            (yup, ym_r, (0, 1, 0)),
+            (zdn, zp_r, (0, 0, -1)),
+            (zup, zm_r, (0, 0, 1)),
+        )
+        return [
+            pltpu.make_async_remote_copy(
+                src_ref=src,
+                dst_ref=dst.at[step],
+                send_sem=face_ss.at[step, i],
+                recv_sem=face_rs.at[step, i],
+                device_id=near(*d),
+                device_id_type=MESH,
+            )
+            for i, (src, dst, d) in enumerate(sends)
+        ]
+
+    sent = [faces(step) for step in range(STEPS)]
+
+    def start_faces(step):
+        for face in sent[step]:
+            face.start()
+
+    def arrive_faces(step):
+        for face in sent[step]:
+            face.wait_recv()
+
+    def leave_faces(step):
+        for face in sent[step]:
+            face.wait_send()
+
+    def pack():
+        for i, c in enumerate((0, 2)):
+            ydn[i] = ef[c, pl.ds(0, CX, stride=CY), :]
+        for c in range(3):
+            yup[c] = ef[c, pl.ds(CY - 1, CX, stride=CY), :]
+            zup[pl.ds(c, 1), :] = to_row(ef[c, :, LANES - 1 : LANES])
+        for c in range(2):
+            zdn[pl.ds(c, 1), :] = to_row(ef[c, :, 0:1])
 
     def edge(cond):
         return jnp.where(cond, 1.0, 0.0).astype(F32)
 
-    e_edge = [edge(ax < n_gx - 1), edge(ay < n_gy - 1), edge(az < n_gz - 1)]
-    h_edge = [edge(ax > 0), edge(ay > 0), edge(az > 0)]
+    top_x, top_y, top_z = edge(ax < n_gx - 1), edge(ay < n_gy - 1), edge(az < n_gz - 1)
+    low_x, low_y, low_z = edge(ax > 0), edge(ay > 0), edge(az > 0)
 
     def spread(face):
         return jnp.broadcast_to(face[:, None, :], (CX, CY, LANES)).reshape(ROWS, LANES)
 
-    def update_h(first):
+    def update_h(step):
         e = [ef[c] for c in range(3)]
-        hx = [ex_r[i] * e_edge[0] if live[0] else jnp.zeros((CY, LANES), F32) for i in range(2)]
-        hy = [ey_r[i] * e_edge[1] if live[1] else jnp.zeros((CX, LANES), F32) for i in range(2)]
-        hz = [
-            to_column(ez_r[pl.ds(i, 1), :]) * e_edge[2] if live[2] else jnp.zeros((ROWS, 1), F32)
-            for i in range(2)
-        ]
-        x1 = jnp.concatenate([e[1][CY:], hx[0]], axis=0)
-        x2 = jnp.concatenate([e[2][CY:], hx[1]], axis=0)
+        xp = [xp_r[step, i] * top_x for i in range(2)]
+        yp = [yp_r[step, i] * top_y for i in range(2)]
+        zp = [to_column(zp_r[step, i : i + 1, :]) * top_z for i in range(2)]
+        x1 = jnp.concatenate([e[1][CY:], xp[0]], axis=0)
+        x2 = jnp.concatenate([e[2][CY:], xp[1]], axis=0)
         last_y = lax.rem(sub, CY) == CY - 1
-        y0 = jnp.where(last_y, spread(hy[0]), pltpu.roll(e[0], ROWS - 1, 0))
-        y2 = jnp.where(last_y, spread(hy[1]), pltpu.roll(e[2], ROWS - 1, 0))
+        y0 = jnp.where(last_y, spread(yp[0]), pltpu.roll(e[0], ROWS - 1, 0))
+        y2 = jnp.where(last_y, spread(yp[1]), pltpu.roll(e[2], ROWS - 1, 0))
         last_z = lane == LANES - 1
-        z0 = jnp.where(last_z, hz[0], pltpu.roll(e[0], LANES - 1, 1))
-        z1 = jnp.where(last_z, hz[1], pltpu.roll(e[1], LANES - 1, 1))
+        z0 = jnp.where(last_z, zp[0], pltpu.roll(e[0], LANES - 1, 1))
+        z1 = jnp.where(last_z, zp[1], pltpu.roll(e[1], LANES - 1, 1))
         curl = (
             (y2 - e[2]) - (z1 - e[1]),
             (z0 - e[0]) - (x2 - e[2]),
             (x1 - e[1]) - (y0 - e[0]),
         )
         for c in range(3):
-            if first:
-                hf[c] = -DT * curl[c]
+            hf[c] = -DT * curl[c] if step == 0 else hf[c] - DT * curl[c]
+
+        e0, e1, e2 = (xm_r[step, c] for c in range(3))
+        sub_x, lane_x = sub[:CY], lane[:CY]
+        corner = jnp.sum(
+            jnp.where(lane_x == sub_x + (ROWS - CY), xz_r[step, 0:1, :], 0.0), axis=1, keepdims=True
+        )
+        z0 = jnp.where(lane_x == LANES - 1, corner * top_z, pltpu.roll(e0, LANES - 1, 1))
+        y0 = jnp.where(
+            sub_x == CY - 1, xy_r[step, 0:1, :] * top_y, pltpu.roll(e0, CY - 1, 0)
+        )
+        curl_x = (
+            (z0 - e0) - (ef[2, 0:CY, :] - e2),
+            (ef[1, 0:CY, :] - e1) - (y0 - e0),
+        )
+
+        e0, e1, e2 = (ym_r[step, c] for c in range(3))
+        sub_y, lane_y = sub[:CX], lane[:CX]
+        corner = jnp.sum(
+            jnp.where(lane_y == sub_y * CY + (CY - 1), yz_r[step, 1:2, :], 0.0),
+            axis=1,
+            keepdims=True,
+        )
+        z1 = jnp.where(lane_y == LANES - 1, corner * top_z, pltpu.roll(e1, LANES - 1, 1))
+        x1 = jnp.where(
+            sub_y == CX - 1, yx_r[step, 7:8, :] * top_x, pltpu.roll(e1, CX - 1, 0)
+        )
+        curl_y = (
+            (ydn[1] - e2) - (z1 - e1),
+            (x1 - e1) - (ydn[0] - e0),
+        )
+
+        below = zm_r[step]
+        e0, e1, e2 = below[0:1], below[1:2], below[2:3]
+        lane_z = lax.broadcasted_iota(jnp.int32, (8, LANES), 1)
+        along = pltpu.roll(zy_r[step], CY - 1, 1) * top_y
+        y2 = jnp.where(
+            lax.rem(lane_z, CY) == CY - 1, along, pltpu.roll(below, LANES - 1, 1)
+        )[2:3]
+        along = pltpu.roll(zx_r[step], ROWS - CY, 1) * top_x
+        x2 = jnp.where(lane_z >= ROWS - CY, along, pltpu.roll(below, LANES - CY, 1))[2:3]
+        curl_z = (
+            (y2 - e2) - (zdn[1:2, :] - e1),
+            (zdn[0:1, :] - e0) - (x2 - e2),
+        )
+        for i in range(2):
+            if step == 0:
+                hx[i] = -DT * curl_x[i]
+                hy[i] = -DT * curl_y[i]
+                hz[i : i + 1, :] = -DT * curl_z[i]
             else:
-                hf[c] = hf[c] - DT * curl[c]
+                hx[i] = hx[i] - DT * curl_x[i]
+                hy[i] = hy[i] - DT * curl_y[i]
+                hz[i : i + 1, :] = hz[i : i + 1, :] - DT * curl_z[i]
 
     def update_e(source):
         h = [hf[c] for c in range(3)]
-        hx = [hx_r[i] * h_edge[0] if live[0] else jnp.zeros((CY, LANES), F32) for i in range(2)]
-        hy = [hy_r[i] * h_edge[1] if live[1] else jnp.zeros((CX, LANES), F32) for i in range(2)]
-        hz = [
-            to_column(hz_r[pl.ds(i, 1), :]) * h_edge[2] if live[2] else jnp.zeros((ROWS, 1), F32)
-            for i in range(2)
-        ]
-        x1 = jnp.concatenate([hx[0], h[1][: ROWS - CY]], axis=0)
-        x2 = jnp.concatenate([hx[1], h[2][: ROWS - CY]], axis=0)
+        xm = [hx[i] * low_x for i in range(2)]
+        ym = [hy[i] * low_y for i in range(2)]
+        zm = [to_column(hz[i : i + 1, :]) * low_z for i in range(2)]
+        x1 = jnp.concatenate([xm[0], h[1][: ROWS - CY]], axis=0)
+        x2 = jnp.concatenate([xm[1], h[2][: ROWS - CY]], axis=0)
         first_y = lax.rem(sub, CY) == 0
-        y0 = jnp.where(first_y, spread(hy[0]), pltpu.roll(h[0], 1, 0))
-        y2 = jnp.where(first_y, spread(hy[1]), pltpu.roll(h[2], 1, 0))
+        y0 = jnp.where(first_y, spread(ym[0]), pltpu.roll(h[0], 1, 0))
+        y2 = jnp.where(first_y, spread(ym[1]), pltpu.roll(h[2], 1, 0))
         first_z = lane == 0
-        z0 = jnp.where(first_z, hz[0], pltpu.roll(h[0], 1, 1))
-        z1 = jnp.where(first_z, hz[1], pltpu.roll(h[1], 1, 1))
+        z0 = jnp.where(first_z, zm[0], pltpu.roll(h[0], 1, 1))
+        z1 = jnp.where(first_z, zm[1], pltpu.roll(h[1], 1, 1))
         curl = (
             (h[2] - y2) - (h[1] - z1),
             (h[0] - z0) - (h[2] - x2),
@@ -440,9 +496,9 @@
             for c in range(3)
         ]
 
-    ez_s[...] = jnp.zeros_like(ez_s)
-    hz_s[...] = jnp.zeros_like(hz_s)
-    pack_e()
+    zdn[...] = jnp.zeros_like(zdn)
+    zup[...] = jnp.zeros_like(zup)
+    pack()
     kind = cls[...]
     inverse = jnp.zeros((ROWS, LANES), F32)
     for number, epsilon in enumerate(EPSILON):
@@ -451,46 +507,41 @@
 
     pl.semaphore_wait(barrier, greetings)
     idx_start()
-    start_faces(e_faces)
+    start_faces(0)
     st_start()
 
     def steps(*accs):
         for step in range(STEPS):
+            last = step == STEPS - 1
             if step == 0:
-                arrive_faces(e_faces)
-                update_h(True)
-                pack_h()
-                start_faces(h_faces)
+                arrive_faces(0)
+                update_h(0)
                 idx_arrive()
                 build()
                 gather(accs)
                 st_arrive()
                 coefficients()
             else:
-                if step == STEPS - 1:
+                if last:
                     early()
                     b0_start()
                 gather(accs)
-                arrive_faces(e_faces)
-                leave_faces(h_faces)
-                update_h(False)
-                pack_h()
-                start_faces(h_faces)
-            changes = bloch(step == STEPS - 1)
-            if step == STEPS - 1:
+            changes = bloch(last)
+            if last:
                 b1_start()
             source = scatter(changes, accs)
-            arrive_faces(h_faces)
-            leave_faces(e_faces)
+            if step:
+                arrive_faces(step)
+                update_h(step)
+            leave_faces(step)
             update_e(source)
-            if step < STEPS - 1:
-                pack_e()
-                start_faces(e_faces)
+            if not last:
+                pack()
+                start_faces(step + 1)
 
     pl.run_scoped(
         steps, *[pltpu.ACC(i % 2)((3 * HALF, 2 * LANES), F32) for i in range(4)]
     )
-    leave_faces(h_faces)
 
     b0_arrive()
     b1_arrive()
@@ -548,15 +599,18 @@
             vmem((6 * HALF, 2 * LANES), BF16),
             vmem((3, *plane), F32),
             vmem((2, CX, LANES), F32),
+            vmem((3, CX, LANES), F32),
             vmem((8, LANES), F32),
-            vmem((2, CX, LANES), F32),
             vmem((8, LANES), F32),
             vmem((2, CY, LANES), F32),
             vmem((2, CX, LANES), F32),
             vmem((8, LANES), F32),
-            vmem((2, CY, LANES), F32),
-            vmem((2, CX, LANES), F32),
-            vmem((8, LANES), F32),
+            vmem((STEPS, 2, CY, LANES), F32),
+            vmem((STEPS, 2, CX, LANES), F32),
+            vmem((STEPS, 8, LANES), F32),
+            vmem((STEPS, 3, CY, LANES), F32),
+            vmem((STEPS, 3, CX, LANES), F32),
+            *[vmem((STEPS, 8, LANES), F32)] * 7,
             dma((9,)),
             dma((4,)),
             dma((group,)),
@@ -567,10 +621,8 @@
             dma((group,)),
             dma((group,)),
             dma((group,)),
-            dma((3,)),
-            dma((3,)),
-            dma((3,)),
-            dma((3,)),
+            dma((STEPS, 12)),
+            dma((STEPS, 12)),
         ],
         compiler_params=pltpu.CompilerParams(collective_id=0, has_side_effects=True),
         name="laser",

time: 47.3 us -> 40.3 us (0.85)
  Pallas kernels: 46.4 us -> 39.5 us
    pallas_call x1, Pallas kernels: 45.6 us -> 38.6 us  [shards(): pl.pallas_call(functools.partial(kernel, sizes), out_shape=(vmem((3, *cel...]
where the time goes in v4:
time: 40.3 us; the launch traced here: 40.1 us
  Pallas kernels  39.5 us (98%)
  between operations  0.64 us (2%)
    pallas_call x1, Pallas kernels, shards(): pl.pallas_call(functools.partial(kernel, sizes), out_shape=(vmem((3, *cel...  38.6 us
    pallas_call x1, Pallas kernels, shards(): pl.pallas_call(write, out_shape=(jax.ShapeDtypeStruct((3, *cell_rows), F3...  0.83 us

profile of v4, /device:TPU:1, one launch (start us, length us, event | category | flops | bytes accessed | tf_op | source)
XLA Modules:
  0.0 40.1 jit_solution(17235297351993893283)
XLA Ops:
  0.6 38.6 %laser.1 = (f32[3,128,128]{2,1,0:T(8,128)S(1)}, f32[3,128,128]{2,1,0:T(8,128)S(1)}, f32[8,32,128]{2,1,0:T(8,128)S(1)}) custom-call(f32[3,128,128]{2,1,0:T(8,128)} %bitcast.17, s32[128,128]{1,0:T(8,128)} %bitcast.19, s32[32,128]{1,0:T(8,128)} %bitcast.21, f32[6,32,128]{2,1,0:T(8,128)} %bitcast.18, f32[2,32,128]{2,1,0:T(8,128)} %bitcast.20, ...), custom_call_target="tpu_custom_call" | custom-call | tf_op jit(solution)/shard_map/laser/pallas_call | solution.py:577
  39.3 0.8 %write.1 = (f32[3,128,128]{2,1,0:T(8,128)}, f32[3,128,128]{2,1,0:T(8,128)}, f32[6,32,128]{2,1,0:T(8,128)}, f32[2,32,128]{2,1,0:T(8,128)}) custom-call(f32[3,128,128]{2,1,0:T(8,128)S(1)} %get-tuple-element.11.ef, f32[3,128,128]{2,1,0:T(8,128)S(1)} %get-tuple-element.12.hf, f32[8,32,128]{2,1,0:T(8,128)S(1)} %get-tuple-element.13.ret), custom_call_target="tpu_custom_call" | custom-call | tf_op jit(solution)/shard_map/write/pallas_call | solution.py:640

commit v5 on v4

--- a/solution.py
+++ b/solution.py
@@ -35,6 +35,22 @@
 def split(x):
     hi = x.astype(BF16)
     return hi, (x - hi.astype(F32)).astype(BF16)
+
+
+PLACE = {}
+HALO = 0
+for name, rows in (
+    ("xp0", CY),
+    ("xp1", CY),
+    ("xm0", CY),
+    ("xm1", CY),
+    ("xm2", CY),
+    ("yp", 2 * CX),
+    ("ym", 3 * CX),
+    *((name, 8) for name in ("zp", "zm", "xz", "xy", "yz", "yx", "zy", "zx")),
+):
+    PLACE[name] = (HALO, rows)
+    HALO += rows
 
 
 def wrap(i, n):
@@ -76,30 +92,10 @@
     hx,
     hy,
     hz,
-    xp_r,
-    yp_r,
-    zp_r,
-    xm_r,
-    ym_r,
-    zm_r,
-    xz_r,
-    xy_r,
-    yz_r,
-    yx_r,
-    zy_r,
-    zx_r,
+    halo,
     load_sem,
-    self_sem,
-    idx_ss,
-    idx_rs,
-    st_ss,
-    st_rs,
-    b0_ss,
-    b0_rs,
-    b1_ss,
-    b1_rs,
-    face_ss,
-    face_rs,
+    group_sem,
+    face_sem,
 ):
     n_gx, n_gy, n_gz = sizes
     group = n_gy * n_gz
@@ -161,48 +157,43 @@
             return buf.at[pl.ds(p, 1), :]
         return buf.at[:, pl.ds(p, 1), :]
 
-    def exchange(src, dst, ss, rs, sem):
-        mine = pltpu.make_async_copy(row(src, me), row(dst, me), sem)
-        out, back = [], []
+    def exchange(src, dst, at):
+        ss, rs = group_sem.at[0, at], group_sem.at[1, at]
+
+        mine = pltpu.make_async_copy(row(src, me), row(dst, me), rs)
+        out = []
         for y, z in peers:
             p = y * n_gz + z
-            ends = ((row(src, p), row(dst, me), rs.at[me]), (row(src, p), row(dst, p), rs.at[p]))
-            for copies, (from_ref, to_ref, recv) in zip((out, back), ends):
-                copies.append(
-                    pltpu.make_async_remote_copy(
-                        src_ref=from_ref,
-                        dst_ref=to_ref,
-                        send_sem=ss.at[p],
-                        recv_sem=recv,
-                        device_id=(ax, y, z),
-                        device_id_type=MESH,
-                    )
+            out.append(
+                pltpu.make_async_remote_copy(
+                    src_ref=row(src, p),
+                    dst_ref=row(dst, me),
+                    send_sem=ss,
+                    recv_sem=rs,
+                    device_id=(ax, y, z),
+                    device_id_type=MESH,
                 )
+            )
+        most = pl.ds(0, group - 1)
+        gone = src.at[most, :] if len(src.shape) == 2 else src.at[:, most, :]
 
         def start():
-            mine.start()
             for copy in out:
                 copy.start()
+            mine.start()
 
         def arrive():
-            mine.wait()
-            for copy in back:
-                copy.wait_recv()
+            pltpu.make_async_copy(dst, dst, rs).wait()
 
         def leave():
-            for copy in out:
-                copy.wait_send()
+            pltpu.make_async_copy(gone, gone, ss).wait()
 
         return start, arrive, leave
 
-    idx_start, idx_arrive, idx_leave = exchange(oidx, sidx, idx_ss, idx_rs, self_sem.at[0])
-    st_start, st_arrive, st_leave = exchange(own, st, st_ss, st_rs, self_sem.at[1])
-    b0_start, b0_arrive, b0_leave = exchange(
-        back.at[pl.ds(0, 4)], ret.at[pl.ds(0, 4)], b0_ss, b0_rs, self_sem.at[2]
-    )
-    b1_start, b1_arrive, b1_leave = exchange(
-        back.at[pl.ds(4, 4)], ret.at[pl.ds(4, 4)], b1_ss, b1_rs, self_sem.at[3]
-    )
+    idx_start, idx_arrive, idx_leave = exchange(oidx, sidx, 0)
+    st_start, st_arrive, st_leave = exchange(own, st, 1)
+    b0_start, b0_arrive, b0_leave = exchange(back.at[pl.ds(0, 4)], ret.at[pl.ds(0, 4)], 2)
+    b1_start, b1_arrive, b1_leave = exchange(back.at[pl.ds(4, 4)], ret.at[pl.ds(4, 4)], 3)
 
     sub = lax.broadcasted_iota(jnp.int32, (ROWS, LANES), 0)
     lane = lax.broadcasted_iota(jnp.int32, (ROWS, LANES), 1)
@@ -215,31 +206,37 @@
         return jnp.sum(jnp.where(eye, line, 0.0), axis=1, keepdims=True)
 
     def faces(step):
-        sends = (
-            (zdn, xz_r, (1, 0, -1)),
-            (ef.at[0, pl.ds(ROWS - CY, 8), :], xy_r, (1, -1, 0)),
-            (zdn, yz_r, (0, 1, -1)),
-            (ef.at[1, pl.ds(CY - 8, 8), :], yx_r, (-1, 1, 0)),
-            (zup, zy_r, (0, -1, 1)),
-            (zup, zx_r, (-1, 0, 1)),
-            (ef.at[pl.ds(1, 2), pl.ds(0, CY), :], xp_r, (-1, 0, 0)),
-            (ef.at[:, pl.ds(ROWS - CY, CY), :], xm_r, (1, 0, 0)),
-            (ydn, yp_r, (0, -1, 0)),
-            (yup, ym_r, (0, 1, 0)),
-            (zdn, zp_r, (0, 0, -1)),
-            (zup, zm_r, (0, 0, 1)),
-        )
+        sends = [
+            (zdn, "xz", (1, 0, -1)),
+            (ef.at[0, pl.ds(ROWS - CY, 8), :], "xy", (1, -1, 0)),
+            (zdn, "yz", (0, 1, -1)),
+            (ef.at[1, pl.ds(CY - 8, 8), :], "yx", (-1, 1, 0)),
+            (zup, "zy", (0, -1, 1)),
+            (zup, "zx", (-1, 0, 1)),
+            (ydn, "yp", (0, -1, 0)),
+            (yup, "ym", (0, 1, 0)),
+            (zdn, "zp", (0, 0, -1)),
+            (zup, "zm", (0, 0, 1)),
+        ]
+        for i in range(2):
+            sends.append((ef.at[1 + i, pl.ds(0, CY), :], f"xp{i}", (-1, 0, 0)))
+        for i in range(3):
+            sends.append((ef.at[i, pl.ds(ROWS - CY, CY), :], f"xm{i}", (1, 0, 0)))
         return [
             pltpu.make_async_remote_copy(
                 src_ref=src,
-                dst_ref=dst.at[step],
-                send_sem=face_ss.at[step, i],
-                recv_sem=face_rs.at[step, i],
+                dst_ref=halo.at[step, pl.ds(*PLACE[name]), :],
+                send_sem=face_sem.at[0, step],
+                recv_sem=face_sem.at[1, step],
                 device_id=near(*d),
                 device_id_type=MESH,
             )
-            for i, (src, dst, d) in enumerate(sends)
+            for src, name, d in sends
         ]
+
+    def got(step, name, first=0, count=None):
+        start, size = PLACE[name]
+        return halo[step, pl.ds(start + first, count or size), :]
 
     sent = [faces(step) for step in range(STEPS)]
 
@@ -248,18 +245,18 @@
             face.start()
 
     def arrive_faces(step):
-        for face in sent[step]:
-            face.wait_recv()
+        whole = halo.at[step]
+        pltpu.make_async_copy(whole, whole, face_sem.at[1, step]).wait()
 
     def leave_faces(step):
-        for face in sent[step]:
-            face.wait_send()
+        whole = halo.at[step]
+        pltpu.make_async_copy(whole, whole, face_sem.at[0, step]).wait()
 
     def pack():
         for i, c in enumerate((0, 2)):
-            ydn[i] = ef[c, pl.ds(0, CX, stride=CY), :]
+            ydn[pl.ds(i * CX, CX), :] = ef[c, pl.ds(0, CX, stride=CY), :]
         for c in range(3):
-            yup[c] = ef[c, pl.ds(CY - 1, CX, stride=CY), :]
+            yup[pl.ds(c * CX, CX), :] = ef[c, pl.ds(CY - 1, CX, stride=CY), :]
             zup[pl.ds(c, 1), :] = to_row(ef[c, :, LANES - 1 : LANES])
         for c in range(2):
             zdn[pl.ds(c, 1), :] = to_row(ef[c, :, 0:1])
@@ -275,9 +272,9 @@
 
     def update_h(step):
         e = [ef[c] for c in range(3)]
-        xp = [xp_r[step, i] * top_x for i in range(2)]
-        yp = [yp_r[step, i] * top_y for i in range(2)]
-        zp = [to_column(zp_r[step, i : i + 1, :]) * top_z for i in range(2)]
+        xp = [got(step, f"xp{i}") * top_x for i in range(2)]
+        yp = [got(step, "yp", i * CX, CX) * top_y for i in range(2)]
+        zp = [to_column(got(step, "zp", i, 1)) * top_z for i in range(2)]
         x1 = jnp.concatenate([e[1][CY:], xp[0]], axis=0)
         x2 = jnp.concatenate([e[2][CY:], xp[1]], axis=0)
         last_y = lax.rem(sub, CY) == CY - 1
@@ -294,44 +291,44 @@
         for c in range(3):
             hf[c] = -DT * curl[c] if step == 0 else hf[c] - DT * curl[c]
 
-        e0, e1, e2 = (xm_r[step, c] for c in range(3))
+        e0, e1, e2 = (got(step, f"xm{c}") for c in range(3))
         sub_x, lane_x = sub[:CY], lane[:CY]
         corner = jnp.sum(
-            jnp.where(lane_x == sub_x + (ROWS - CY), xz_r[step, 0:1, :], 0.0), axis=1, keepdims=True
+            jnp.where(lane_x == sub_x + (ROWS - CY), got(step, "xz", 0, 1), 0.0), axis=1, keepdims=True
         )
         z0 = jnp.where(lane_x == LANES - 1, corner * top_z, pltpu.roll(e0, LANES - 1, 1))
         y0 = jnp.where(
-            sub_x == CY - 1, xy_r[step, 0:1, :] * top_y, pltpu.roll(e0, CY - 1, 0)
+            sub_x == CY - 1, got(step, "xy", 0, 1) * top_y, pltpu.roll(e0, CY - 1, 0)
         )
         curl_x = (
             (z0 - e0) - (ef[2, 0:CY, :] - e2),
             (ef[1, 0:CY, :] - e1) - (y0 - e0),
         )
 
-        e0, e1, e2 = (ym_r[step, c] for c in range(3))
+        e0, e1, e2 = (got(step, "ym", c * CX, CX) for c in range(3))
         sub_y, lane_y = sub[:CX], lane[:CX]
         corner = jnp.sum(
-            jnp.where(lane_y == sub_y * CY + (CY - 1), yz_r[step, 1:2, :], 0.0),
+            jnp.where(lane_y == sub_y * CY + (CY - 1), got(step, "yz", 1, 1), 0.0),
             axis=1,
             keepdims=True,
         )
         z1 = jnp.where(lane_y == LANES - 1, corner * top_z, pltpu.roll(e1, LANES - 1, 1))
         x1 = jnp.where(
-            sub_y == CX - 1, yx_r[step, 7:8, :] * top_x, pltpu.roll(e1, CX - 1, 0)
+            sub_y == CX - 1, got(step, "yx", 7, 1) * top_x, pltpu.roll(e1, CX - 1, 0)
         )
         curl_y = (
-            (ydn[1] - e2) - (z1 - e1),
-            (x1 - e1) - (ydn[0] - e0),
-        )
-
-        below = zm_r[step]
+            (ydn[CX : 2 * CX, :] - e2) - (z1 - e1),
+            (x1 - e1) - (ydn[0:CX, :] - e0),
+        )
+
+        below = got(step, "zm")
         e0, e1, e2 = below[0:1], below[1:2], below[2:3]
         lane_z = lax.broadcasted_iota(jnp.int32, (8, LANES), 1)
-        along = pltpu.roll(zy_r[step], CY - 1, 1) * top_y
+        along = pltpu.roll(got(step, "zy"), CY - 1, 1) * top_y
         y2 = jnp.where(
             lax.rem(lane_z, CY) == CY - 1, along, pltpu.roll(below, LANES - 1, 1)
         )[2:3]
-        along = pltpu.roll(zx_r[step], ROWS - CY, 1) * top_x
+        along = pltpu.roll(got(step, "zx"), ROWS - CY, 1) * top_x
         x2 = jnp.where(lane_z >= ROWS - CY, along, pltpu.roll(below, LANES - CY, 1))[2:3]
         curl_z = (
             (y2 - e2) - (zdn[1:2, :] - e1),
@@ -534,6 +531,9 @@
                 arrive_faces(step)
                 update_h(step)
             leave_faces(step)
+            if step == 1:
+                idx_leave()
+                st_leave()
             update_e(source)
             if not last:
                 pack()
@@ -545,8 +545,6 @@
 
     b0_arrive()
     b1_arrive()
-    idx_leave()
-    st_leave()
     b0_leave()
     b1_leave()
 
@@ -598,31 +596,17 @@
             vmem((HALF, group * LANES), BF16),
             vmem((6 * HALF, 2 * LANES), BF16),
             vmem((3, *plane), F32),
-            vmem((2, CX, LANES), F32),
-            vmem((3, CX, LANES), F32),
+            vmem((2 * CX, LANES), F32),
+            vmem((3 * CX, LANES), F32),
             vmem((8, LANES), F32),
             vmem((8, LANES), F32),
             vmem((2, CY, LANES), F32),
             vmem((2, CX, LANES), F32),
             vmem((8, LANES), F32),
-            vmem((STEPS, 2, CY, LANES), F32),
-            vmem((STEPS, 2, CX, LANES), F32),
-            vmem((STEPS, 8, LANES), F32),
-            vmem((STEPS, 3, CY, LANES), F32),
-            vmem((STEPS, 3, CX, LANES), F32),
-            *[vmem((STEPS, 8, LANES), F32)] * 7,
+            vmem((STEPS, HALO, LANES), F32),
             dma((9,)),
-            dma((4,)),
-            dma((group,)),
-            dma((group,)),
-            dma((group,)),
-            dma((group,)),
-            dma((group,)),
-            dma((group,)),
-            dma((group,)),
-            dma((group,)),
-            dma((STEPS, 12)),
-            dma((STEPS, 12)),
+            dma((2, 4)),
+            dma((2, STEPS)),
         ],
         compiler_params=pltpu.CompilerParams(collective_id=0, has_side_effects=True),
         name="laser",

time: 40.3 us -> 36.9 us (0.916)
  Pallas kernels: 39.5 us -> 36.1 us
    pallas_call x1, Pallas kernels: 38.6 us -> 35.3 us  [shards(): pl.pallas_call(functools.partial(kernel, sizes), out_shape=(vmem((3, *cel...]
where the time goes in v5:
time: 36.9 us; the launch traced here: 36.7 us
  Pallas kernels  36.1 us (98%)
  between operations  0.64 us (2%)
    pallas_call x1, Pallas kernels, shards(): pl.pallas_call(functools.partial(kernel, sizes), out_shape=(vmem((3, *cel...  35.3 us
    pallas_call x1, Pallas kernels, shards(): pl.pallas_call(write, out_shape=(jax.ShapeDtypeStruct((3, *cell_rows), F3...  0.83 us

profile of v5, /device:TPU:1, one launch (start us, length us, event | category | flops | bytes accessed | tf_op | source)
XLA Modules:
  0.0 36.7 jit_solution(4661335257381445770)
XLA Ops:
  0.6 35.3 %laser.1 = (f32[3,128,128]{2,1,0:T(8,128)S(1)}, f32[3,128,128]{2,1,0:T(8,128)S(1)}, f32[8,32,128]{2,1,0:T(8,128)S(1)}) custom-call(f32[3,128,128]{2,1,0:T(8,128)} %bitcast.17, s32[128,128]{1,0:T(8,128)} %bitcast.19, s32[32,128]{1,0:T(8,128)} %bitcast.21, f32[6,32,128]{2,1,0:T(8,128)} %bitcast.18, f32[2,32,128]{2,1,0:T(8,128)} %bitcast.20, ...), custom_call_target="tpu_custom_call" | custom-call | tf_op jit(solution)/shard_map/laser/pallas_call | solution.py:575
  35.9 0.8 %write.1 = (f32[3,128,128]{2,1,0:T(8,128)}, f32[3,128,128]{2,1,0:T(8,128)}, f32[6,32,128]{2,1,0:T(8,128)}, f32[2,32,128]{2,1,0:T(8,128)}) custom-call(f32[3,128,128]{2,1,0:T(8,128)S(1)} %get-tuple-element.11.ef, f32[3,128,128]{2,1,0:T(8,128)S(1)} %get-tuple-element.12.hf, f32[8,32,128]{2,1,0:T(8,128)S(1)} %get-tuple-element.13.ret), custom_call_target="tpu_custom_call" | custom-call | tf_op jit(solution)/shard_map/write/pallas_call | solution.py:624

commit v6 on v5

--- a/solution.py
+++ b/solution.py
@@ -81,7 +81,6 @@
     coef,
     qsel,
     wide,
-    tall,
     pick,
     el,
     samp,
@@ -370,18 +369,11 @@
         key = ((cell >> 13) << 7) | (cell & (LANES - 1))
         quo = (cell >> 7) & (HALF - 1)
         qsel[...] = quo
-        key_t = jnp.transpose(
-            jnp.concatenate([key, jnp.zeros((LANES - group, LANES), jnp.int32)], axis=0)
-            if group < LANES
-            else key
-        )
         down_256 = lax.broadcasted_iota(jnp.int32, (2 * LANES, LANES), 0)
-        across_256 = lax.broadcasted_iota(jnp.int32, (LANES, 2 * LANES), 1)
         down_64 = lax.broadcasted_iota(jnp.int32, (HALF, LANES), 0)
         for b in range(group):
             where = pl.ds(b * LANES, LANES)
             wide[:, where] = jnp.where(down_256 == key[b : b + 1, :], 1.0, 0.0).astype(BF16)
-            tall[where, :] = jnp.where(across_256 == key_t[:, b : b + 1], 1.0, 0.0).astype(BF16)
             pick[:, where] = jnp.where(down_64 == quo[b : b + 1, :], 1.0, 0.0).astype(BF16)
 
     def coefficients():
@@ -461,7 +453,9 @@
         parts = [[part[piece].astype(F32) for part in parts] for piece in range(2)]
         for t in range(group // 2):
             mxu, reg, acc = t % 2, (t // 2) % 2, accs[t % 2]
-            pltpu.matmul_push_rhs(tall[pl.ds(t * 2 * LANES, 2 * LANES), :], reg, mxu)
+            pltpu.matmul_push_rhs(
+                wide[:, pl.ds(t * 2 * LANES, 2 * LANES)], reg, mxu, transpose=True
+            )
             for piece in range(2):
                 rows = []
                 for c in range(3):
@@ -592,7 +586,6 @@
             vmem((4, *plane), F32),
             vmem(plane, jnp.int32),
             vmem((2 * LANES, group * LANES), BF16),
-            vmem((group * LANES, 2 * LANES), BF16),
             vmem((HALF, group * LANES), BF16),
             vmem((6 * HALF, 2 * LANES), BF16),
             vmem((3, *plane), F32),

time: 36.9 us -> 36.1 us (0.978)
  Pallas kernels: 36.1 us -> 35.2 us
    pallas_call x1, Pallas kernels: 35.3 us -> 34.4 us  [shards(): pl.pallas_call(functools.partial(kernel, sizes), out_shape=(vmem((3, *cel...]
where the time goes in v6:
time: 36.1 us; the launch traced here: 35.9 us
  Pallas kernels  35.2 us (98%)
  between operations  0.64 us (2%)
    pallas_call x1, Pallas kernels, shards(): pl.pallas_call(functools.partial(kernel, sizes), out_shape=(vmem((3, *cel...  34.4 us
    pallas_call x1, Pallas kernels, shards(): pl.pallas_call(write, out_shape=(jax.ShapeDtypeStruct((3, *cell_rows), F3...  0.83 us

profile of v6, /device:TPU:1, one launch (start us, length us, event | category | flops | bytes accessed | tf_op | source)
XLA Modules:
  0.0 35.9 jit_solution(8022491790056336865)
XLA Ops:
  0.6 34.4 %laser.1 = (f32[3,128,128]{2,1,0:T(8,128)S(1)}, f32[3,128,128]{2,1,0:T(8,128)S(1)}, f32[8,32,128]{2,1,0:T(8,128)S(1)}) custom-call(f32[3,128,128]{2,1,0:T(8,128)} %bitcast.17, s32[128,128]{1,0:T(8,128)} %bitcast.19, s32[32,128]{1,0:T(8,128)} %bitcast.21, f32[6,32,128]{2,1,0:T(8,128)} %bitcast.18, f32[2,32,128]{2,1,0:T(8,128)} %bitcast.20, ...), custom_call_target="tpu_custom_call" | custom-call | tf_op jit(solution)/shard_map/laser/pallas_call | solution.py:569
  35.1 0.8 %write.1 = (f32[3,128,128]{2,1,0:T(8,128)}, f32[3,128,128]{2,1,0:T(8,128)}, f32[6,32,128]{2,1,0:T(8,128)}, f32[2,32,128]{2,1,0:T(8,128)}) custom-call(f32[3,128,128]{2,1,0:T(8,128)S(1)} %get-tuple-element.11.ef, f32[3,128,128]{2,1,0:T(8,128)S(1)} %get-tuple-element.12.hf, f32[8,32,128]{2,1,0:T(8,128)S(1)} %get-tuple-element.13.ret), custom_call_target="tpu_custom_call" | custom-call | tf_op jit(solution)/shard_map/write/pallas_call | solution.py:617

commit v7 on v6

--- a/solution.py
+++ b/solution.py
@@ -369,11 +369,15 @@
         key = ((cell >> 13) << 7) | (cell & (LANES - 1))
         quo = (cell >> 7) & (HALF - 1)
         qsel[...] = quo
-        down_256 = lax.broadcasted_iota(jnp.int32, (2 * LANES, LANES), 0)
+        down_256 = lax.broadcasted_iota(jnp.int32, (2 * LANES, LANES), 0).astype(F32).astype(BF16)
+        one = jnp.ones((2 * LANES, LANES), BF16)
+        none = jnp.zeros((2 * LANES, LANES), BF16)
         down_64 = lax.broadcasted_iota(jnp.int32, (HALF, LANES), 0)
         for b in range(group):
             where = pl.ds(b * LANES, LANES)
-            wide[:, where] = jnp.where(down_256 == key[b : b + 1, :], 1.0, 0.0).astype(BF16)
+            line = jnp.broadcast_to(key[b : b + 1, :].astype(F32), (CY, LANES)).astype(BF16)
+            line = jnp.concatenate([line] * (2 * LANES // CY), axis=0)
+            wide[:, where] = jnp.where(down_256 == line, one, none)
             pick[:, where] = jnp.where(down_64 == quo[b : b + 1, :], 1.0, 0.0).astype(BF16)
 
     def coefficients():

time: 36.1 us -> 35.8 us (level)
  no operation moved by 1% of the time
where the time goes in v7:
time: 35.8 us; the launch traced here: 35.6 us
  Pallas kernels  35 us (98%)
  between operations  0.64 us (2%)
    pallas_call x1, Pallas kernels, shards(): pl.pallas_call(functools.partial(kernel, sizes), out_shape=(vmem((3, *cel...  34.1 us
    pallas_call x1, Pallas kernels, shards(): pl.pallas_call(write, out_shape=(jax.ShapeDtypeStruct((3, *cell_rows), F3...  0.83 us

profile of v7, /device:TPU:1, one launch (start us, length us, event | category | flops | bytes accessed | tf_op | source)
XLA Modules:
  0.0 35.6 jit_solution(414934445798575818)
XLA Ops:
  0.6 34.1 %laser.1 = (f32[3,128,128]{2,1,0:T(8,128)S(1)}, f32[3,128,128]{2,1,0:T(8,128)S(1)}, f32[8,32,128]{2,1,0:T(8,128)S(1)}) custom-call(f32[3,128,128]{2,1,0:T(8,128)} %bitcast.17, s32[128,128]{1,0:T(8,128)} %bitcast.19, s32[32,128]{1,0:T(8,128)} %bitcast.21, f32[6,32,128]{2,1,0:T(8,128)} %bitcast.18, f32[2,32,128]{2,1,0:T(8,128)} %bitcast.20, ...), custom_call_target="tpu_custom_call" | custom-call | tf_op jit(solution)/shard_map/laser/pallas_call | solution.py:573
  34.8 0.8 %write.1 = (f32[3,128,128]{2,1,0:T(8,128)}, f32[3,128,128]{2,1,0:T(8,128)}, f32[6,32,128]{2,1,0:T(8,128)}, f32[2,32,128]{2,1,0:T(8,128)}) custom-call(f32[3,128,128]{2,1,0:T(8,128)S(1)} %get-tuple-element.11.ef, f32[3,128,128]{2,1,0:T(8,128)S(1)} %get-tuple-element.12.hf, f32[8,32,128]{2,1,0:T(8,128)S(1)} %get-tuple-element.13.ret), custom_call_target="tpu_custom_call" | custom-call | tf_op jit(solution)/shard_map/write/pallas_call | solution.py:621
